TPU v7x, 256 devices: a whole 4x4x8 slice. The times are simulated.
256 devices in a mesh: chan: 32 (over x_hi, z, core), win: 8 (over y, x_lo).
Axes of the slice: x: 4 (x_hi: 2, x_lo: 2; x = x_hi * 2 + x_lo), y: 4, z: 8, core: 2. Of those that a mesh axis runs over, the one named last changes fastest.
Arguments:
- spectra: bfloat16 [2, 16, 4096, 4096], P(None, 'win', 'chan'), may hold values from -6 to 6
- exponents: int32 [16, 4096, 32], P('win', 'chan'), may hold values from -1 to 1
- source_channels: int32 [1], replicated, may hold values from 0 to 4095
Outputs:
- correlations: float32 [1, 4096, 2048], P(None, 'chan', 'win')
All inputs are finite; a program needn't handle non-finite values.
Results may differ from a plain program's by a relative error of at most 0.0003.
Values sent between devices are 32-bit elements; how exact they have to be, the bound alone decides.
No kernel may reach another device: no remote copies, remote signals or barrier semaphores. Data moves between devices by JAX's collectives and lax.ppermute only.
A program may use at most 64 MiB of HBM per device.

v0:
```python
import math

import jax
import jax.numpy as jnp
from jax import lax
from jax.sharding import PartitionSpec as P

L = 2048


def cut_along(array, dim, peers):
    before, after = (array.shape[:dim], array.shape[dim + 1 :])
    return jnp.moveaxis(array.reshape(*before, peers, -1, *after), dim, 0)


def sent_and_summed(array, axis, dim):
    peers = lax.axis_size(axis)
    tiles = lax.all_to_all(cut_along(array, dim, peers), axis, 0, 0, tiled=True)
    return jnp.sum(tiles, axis=0)


def filled_up(lines, peers):
    spare = -lines.shape[0] % peers
    if not spare:
        return lines
    return jnp.concatenate([lines, jnp.zeros((spare, *lines.shape[1:]), lines.dtype)])


def in_order(tiles, dim):
    shape = list(tiles.shape[1:])
    shape[dim] *= tiles.shape[0]
    return jnp.moveaxis(tiles, 0, dim).reshape(shape)


def copy_for_each(array, axis):
    peers = lax.axis_size(axis)
    return lax.all_to_all(
        jnp.broadcast_to(array[None], (peers, *array.shape)), axis, 0, 0, tiled=True
    )


def collect(array, axis, dim):
    return in_order(copy_for_each(array, axis), dim)


def total_of(array, axes):
    lines = array.reshape(-1)
    own = sent_and_summed(filled_up(lines, lax.axis_size(axes)), axes, 0)
    whole = collect(own, axes, 0)
    return whole[: len(lines)].reshape(array.shape)


def dequantize(spectra, exponents, block):
    scale = jnp.exp2(exponents.astype(jnp.float32))
    scale = jnp.repeat(scale, block, axis=2)
    return spectra.astype(jnp.float32) * scale[None]


def phase_table(first, second, period):
    index_one = jnp.arange(first, dtype=jnp.int32)
    index_two = jnp.arange(second, dtype=jnp.int32)
    phase = index_one[:, None] * index_two[None, :] % period
    angle = phase.astype(jnp.float32) * (2.0 * math.pi / period)
    return (jnp.cos(angle), jnp.sin(angle))


def to_lags(real_rows, imag_rows, nbin, block, total_lags, norm):
    high = lax.Precision.HIGHEST
    rows = real_rows.shape[0]
    period = 2 * nbin
    outer = 2 * block
    inner = period // outer
    half = outer // 2
    real_cube = real_rows.reshape(rows, half, inner)
    imag_cube = imag_rows.reshape(rows, half, inner)
    cos_one, sin_one = phase_table(half, outer, outer)
    section_real = jnp.einsum("maq,ap->mpq", real_cube, cos_one, precision=high) - jnp.einsum(
        "maq,ap->mpq", imag_cube, sin_one, precision=high
    )
    section_imag = jnp.einsum("maq,ap->mpq", real_cube, sin_one, precision=high) + jnp.einsum(
        "maq,ap->mpq", imag_cube, cos_one, precision=high
    )
    twiddle_cos, twiddle_sin = phase_table(outer, inner, period)
    turned_real = section_real * twiddle_cos[None] - section_imag * twiddle_sin[None]
    turned_imag = section_real * twiddle_sin[None] + section_imag * twiddle_cos[None]
    cos_two, sin_two = phase_table(inner, inner, inner)
    final = jnp.einsum("mpq,qk->mkp", turned_real, cos_two, precision=high) - jnp.einsum(
        "mpq,qk->mkp", turned_imag, sin_two, precision=high
    )
    flat = final.reshape(rows, period)
    lagged = jnp.concatenate(
        [flat[:, period - total_lags // 2 :], flat[:, : total_lags // 2]], axis=1
    )
    return lagged * norm


def body(spectra, exponents, source_channels):
    nbin = spectra.shape[3]
    block = nbin // exponents.shape[2]
    segs = spectra.shape[1]
    local_count = spectra.shape[2]
    sources = source_channels.shape[0]
    values = dequantize(spectra, exponents, block)
    offset = lax.axis_index("chan") * local_count
    local_index = source_channels - offset
    owned = (local_index >= 0) & (local_index < local_count)
    clipped = jnp.clip(local_index, 0, local_count - 1)
    picked = jnp.take(values, clipped, axis=2)
    masked = picked * owned.astype(jnp.float32)[None, None, :, None]
    slab = total_of(masked, "chan")
    high = lax.Precision.HIGHEST
    real_part = jnp.einsum("gsf,gcf->scf", slab[0], values[0], precision=high) + jnp.einsum(
        "gsf,gcf->scf", slab[1], values[1], precision=high
    )
    imag_part = jnp.einsum("gsf,gcf->scf", slab[0], values[1], precision=high) - jnp.einsum(
        "gsf,gcf->scf", slab[1], values[0], precision=high
    )
    cross = jnp.concatenate([real_part, imag_part], axis=2)
    norm = 1.0 / math.sqrt(4.0 * nbin * segs * lax.axis_size("win"))
    flat = cross.reshape(sources * local_count, 2 * nbin)
    partial_lags = to_lags(flat[:, :nbin], flat[:, nbin:], nbin, block, L, norm)
    partial_lags = partial_lags.reshape(sources, local_count, L)
    return sent_and_summed(partial_lags, "win", 2)


def solution(mesh):
    return jax.shard_map(
        body,
        mesh=mesh,
        in_specs=(P(None, "win", "chan", None), P("win", "chan", None), P()),
        out_specs=P(None, "chan", "win"),
        check_vma=False,
    )
```

profile of v0, /device:TPU:4, one launch (start us, length us, event | category | flops | bytes accessed | tf_op | source)
XLA Modules:
  0.0 168.0 jit_solution(5436097475106580233)
XLA Ops:
  0.7 0.8 multiply_exponential_fusion
  1.4 0.1 copy.22
  1.5 2.6 %broadcast_in_dim.16 = f32[2,128,32,128]{3,2,1,0:T(8,128)} broadcast(f32[2,128,32]{2,1,0:T(8,128)S(1)} %copy.22), dimensions={0,1,2} | broadcast | bytes 4227072 | tf_op jit(solution)/shard_map/broadcast_in_dim | solution.py:55
  4.1 5.0 %mul.227 = f32[2,128,4096]{2,1,0:T(8,128)} reshape(f32[2,128,32,128]{3,2,1,0:T(8,128)} %broadcast_in_dim.16) | data formatting | bytes 8388608 | tf_op jit(solution)/shard_map/mul | solution.py:56
  9.1 4.6 %convert_multiply_fusion = f32[2,2,128,4096]{3,2,1,0:T(8,128)S(1)} fusion(bf16[2,2,128,4096]{3,2,1,0:T(8,128)(2,1)} %param.3, f32[2,128,4096]{2,1,0:T(8,128)} %mul.227), kind=kLoop, calls=%fused_computation | loop fusion | flops 4194304 | bytes 16777216 | tf_op jit(solution)/shard_map/mul | solution.py:56
  13.7 0.0 copy-start
  13.7 3.2 %copy-done = f32[2,2,128,4096]{3,2,1,0:T(8,128)} copy-done((f32[2,2,128,4096]{3,2,1,0:T(8,128)}, f32[2,2,128,4096]{3,2,1,0:T(8,128)S(1)}, u32[]{:S(2)}) %copy-start) | copy-done | bytes 8388632
  16.9 0.1 fusion.12
  17.0 19.2 %all_to_all.17 = f32[32,1,512]{2,1,0:T(1,128)S(1)} all-to-all(f32[32,1,512]{2,1,0:T(1,128)S(1)} %bitcast.82), channel_id=1, replica_groups=mesh['chan'=32,'win'=8] {'chan'}, dimensions={0} | all-to-all | bytes 131072 | tf_op jit(solution)/shard_map/all_to_all | solution.py:18
  36.1 0.1 reduce_sum.20
  36.2 0.7 broadcast_in_dim.20
  36.9 6.6 %all-to-all-start.1 = ((f32[32,1,512]{2,1,0:T(1,128)}), f32[32,1,512]{2,1,0:T(1,128)S(1)}, u32[]{:S(2)}, u32[]{:S(2)}) async-start(f32[32,1,512]{2,1,0:T(1,128)} %broadcast_in_dim.20), calls=%async_computation.1 | async-start | bytes 131072 | tf_op jit(solution)/shard_map/all_to_all | solution.py:37
  43.5 0.1 fusion.32
  43.7 7.6 %all-to-all-done.1 = f32[32,1,512]{2,1,0:T(1,128)S(1)} async-done(((f32[32,1,512]{2,1,0:T(1,128)}), f32[32,1,512]{2,1,0:T(1,128)S(1)}, u32[]{:S(2)}, u32[]{:S(2)}) %all-to-all-start.1) | async-done | bytes 65568 | tf_op jit(solution)/shard_map/all_to_all | solution.py:37
  51.2 0.2 slice_reduce_fusion
  51.5 8.2 %multiply_reduce_fusion.2 = (f32[4096,128]{0,1:T(8,128)}, f32[4096,128]{0,1:T(8,128)}, f32[4096,128]{0,1:T(8,128)}, f32[4096,128]{0,1:T(8,128)}) fusion(f32[2,2,128,4096]{3,2,1,0:T(8,128)} %copy-done, f32[4096,2]{0,1:T(2,128)S(1)} %bitcast.84, f32[4096,2]{0,1:T(2,128)S(1)} %bitcast.83), kind=kLoop, calls=%fused_computation.6 | loop fusion | flops 6291456 | bytes 16842752
  59.7 1.9 %copy.39 = f32[4096,128]{1,0:T(8,128)S(1)} copy(f32[4096,128]{0,1:T(8,128)} %get-tuple-element.21) | data formatting | bytes 4194304 | tf_op jit(solution)/shard_map/gsf,gcf->scf/dot_general | solution.py:112
  61.6 2.9 %copy.46 = f32[4096,128]{1,0:T(8,128)} copy(f32[4096,128]{0,1:T(8,128)} %get-tuple-element.16) | data formatting | bytes 4194304 | tf_op jit(solution)/shard_map/gsf,gcf->scf/dot_general | solution.py:112
  64.5 2.9 %copy.53 = f32[4096,128]{1,0:T(8,128)} copy(f32[4096,128]{0,1:T(8,128)} %get-tuple-element.20) | data formatting | bytes 4194304 | tf_op jit(solution)/shard_map/gsf,gcf->scf/dot_general | solution.py:115
  67.4 2.9 %copy.60 = f32[4096,128]{1,0:T(8,128)} copy(f32[4096,128]{0,1:T(8,128)} %get-tuple-element.17) | data formatting | bytes 4194304 | tf_op jit(solution)/shard_map/gsf,gcf->scf/dot_general | solution.py:115
  70.3 3.3 %subtract_bitcast_fusion.2 = (f32[1,128,4096]{1,2,0:T(8,128)S(1)}, f32[1,128,4096]{1,2,0:T(8,128)S(1)}) fusion(f32[4096,128]{1,0:T(8,128)} %copy.53, f32[4096,128]{1,0:T(8,128)} %copy.60, f32[4096,128]{1,0:T(8,128)S(1)} %copy.39, f32[4096,128]{1,0:T(8,128)} %copy.46), kind=kLoop, calls=%fused_computation.13 | loop fusion | flops 1048576 | bytes 12582912 | tf_op jit(solution)/shard_map/sub | solution.py:115
  73.6 0.3 maximum_bitcast_fusion
  73.9 2.2 %fusion.65 = (f32[128,4096]{0,1:T(8,128)}, f32[128,4096]{0,1:T(8,128)}) fusion(f32[128,8192]{0,1:T(8,128)S(1)} %maximum_bitcast_fusion), kind=kLoop, calls=%fused_computation.88 | loop fusion | bytes 8388608 | tf_op jit(solution)/shard_map/slice | solution.py:121
  76.1 2.0 %copy.24 = f32[128,128,32]{1,0,2:T(8,128)S(1)} copy(f32[128,128,32]{0,2,1:T(8,128)} %bitcast.79) | data formatting | bytes 4194304 | tf_op jit(solution)/shard_map/reshape | solution.py:74
  78.1 5.9 %fusion.3 = f32[256,128,32]{1,0,2:T(8,128)} fusion(f32[128,128,32]{1,0,2:T(8,128)S(1)} %copy.24), kind=kOutput, calls=%fused_computation.22 | convolution fusion | flops 1611071488 | bytes 6291456 | tf_op jit(solution)/shard_map/maq,ap->mpq/dot_general | solution.py:80
  84.0 5.9 %fusion.7 = f32[256,128,32]{1,0,2:T(8,128)} fusion(f32[128,128,32]{1,0,2:T(8,128)S(1)} %copy.24), kind=kOutput, calls=%fused_computation.26 | convolution fusion | flops 1611071488 | bytes 6291456 | tf_op jit(solution)/shard_map/maq,ap->mpq/dot_general | solution.py:77
  89.9 2.0 %copy.25 = f32[128,128,32]{1,0,2:T(8,128)S(1)} copy(f32[128,128,32]{0,2,1:T(8,128)} %bitcast.78) | data formatting | bytes 4194304 | tf_op jit(solution)/shard_map/reshape | solution.py:75
  91.9 0.0 copy-start.1
  91.9 6.4 %convolution_add_fusion = f32[256,128,32]{1,0,2:T(8,128)S(1)} fusion(f32[256,128,32]{1,0,2:T(8,128)} %fusion.3, f32[128,128,32]{1,0,2:T(8,128)S(1)} %copy.25), kind=kOutput, calls=%fused_computation.11 | convolution fusion | flops 1612120064 | bytes 10485760 | tf_op jit(solution)/shard_map/maq,ap->mpq/dot_general | solution.py:80
  98.3 0.0 copy-done.1
  98.4 13.3 %add_bitcast_fusion = (f32[128,256,32]{0,1,2:T(8,128)}, f32[128,256,32]{0,1,2:T(8,128)}) fusion(f32[256,128,32]{1,0,2:T(8,128)S(1)} %convolution_add_fusion, f32[256,32]{0,1:T(8,128)S(1)} %get-tuple-element.32, f32[256,32]{0,1:T(8,128)S(1)} %get-tuple-element.33, f32[256,128,32]{1,0,2:T(8,128)S(1)} %copy-done.1, f32[128,128,32]{1,0,2:T(8,128)S(1)} %copy.25), kind=kOutput, calls=%fused_computation.9 | convolution fusion | flops 1618411520 | bytes 18939904 | tf_op jit(solution)/shard_map/maq,ap->mpq/dot_general | solution.py:77
  111.6 5.5 %copy.28 = f32[128,256,32]{1,2,0:T(8,128)} copy(f32[128,256,32]{0,1,2:T(8,128)} %get-tuple-element.25) | data formatting | bytes 8388608 | tf_op jit(solution)/shard_map/sub | solution.py:84
  117.1 7.9 %fusion.29 = f32[32,128,256]{2,0,1:T(8,128)} fusion(f32[128,256,32]{1,2,0:T(8,128)} %copy.28), kind=kOutput, calls=%fused_computation.54 | convolution fusion | flops 402667520 | bytes 8388608 | tf_op jit(solution)/shard_map/mpq,qk->mkp/dot_general | solution.py:87
  124.9 5.5 %copy.29 = f32[128,256,32]{1,2,0:T(8,128)} copy(f32[128,256,32]{0,1,2:T(8,128)} %get-tuple-element.24) | data formatting | bytes 8388608 | tf_op jit(solution)/shard_map/add | solution.py:85
  130.4 9.2 %subtract_bitcast_fusion = f32[128,32,256]{2,1,0:T(8,128)} fusion(f32[32,128,256]{2,0,1:T(8,128)} %fusion.29, f32[128,256,32]{1,2,0:T(8,128)} %copy.29), kind=kOutput, calls=%fused_computation.8 | convolution fusion | flops 403716096 | bytes 12582912 | tf_op jit(solution)/shard_map/mpq,qk->mkp/dot_general | solution.py:87
  139.6 5.3 %copy.61 = f32[128,32,256]{0,2,1:T(8,128)} copy(f32[128,32,256]{2,1,0:T(8,128)} %subtract_bitcast_fusion) | data formatting | bytes 8388608 | tf_op jit(solution)/shard_map/reshape | solution.py:90
  144.9 1.3 fusion.64
  146.2 0.1 maximum_multiply_fusion
  146.2 0.3 copy.32
  146.6 20.7 %all_to_all.18 = f32[8,1,128,256]{3,2,1,0:T(8,128)S(1)} all-to-all(f32[8,1,128,256]{3,2,1,0:T(8,128)S(1)} %copy.32), channel_id=1, replica_groups=mesh['chan'=32,'win'=8] {'win'}, dimensions={0} | all-to-all | bytes 2097152 | tf_op jit(solution)/shard_map/all_to_all | solution.py:18
  167.3 0.7 reduce_sum.21
  (2 shorter events, 0.1 us)
Async XLA Ops:
  13.7 3.2 %copy-start = (f32[2,2,128,4096]{3,2,1,0:T(8,128)}, f32[2,2,128,4096]{3,2,1,0:T(8,128)S(1)}, u32[]{:S(2)}) copy-start(f32[2,2,128,4096]{3,2,1,0:T(8,128)S(1)} %convert_multiply_fusion) | copy-start | bytes 25165828
  36.9 14.3 %all-to-all-start.1 = ((f32[32,1,512]{2,1,0:T(1,128)}), f32[32,1,512]{2,1,0:T(1,128)S(1)}, u32[]{:S(2)}, u32[]{:S(2)}) async-start(f32[32,1,512]{2,1,0:T(1,128)} %broadcast_in_dim.20), calls=%async_computation.1 | async-start | bytes 131072 | tf_op jit(solution)/shard_map/all_to_all | solution.py:37
  91.9 6.4 %copy-start.1 = (f32[256,128,32]{1,0,2:T(8,128)S(1)}, f32[256,128,32]{1,0,2:T(8,128)}, u32[]{:S(2)}) copy-start(f32[256,128,32]{1,0,2:T(8,128)} %fusion.7) | copy-start | bytes 12582916
where the time goes:
time: 170 us; the launch traced here: 168 us
  matrix products  48.4 us (28%)
  local copies, waits for them, and re-layouts  46.5 us (27%)
  blocking collectives  39.9 us (23%)
  other arithmetic  18.2 us (11%)
  waiting for transfers between devices  7.57 us (4%)
  starting transfers between devices  6.61 us (4%)
    all_to_all x2, blocking collectives, sent_and_summed(): tiles = lax.all_to_all(cut_along(array, dim, peers), axis, 0, 0, tiled=True)  39.9 us
    dot_general x1, matrix products, to_lags(): jnp.einsum('maq,ap->mpq', imag_cube, sin_one, precision=high)  13.3 us
    dot_general x1, matrix products, to_lags(): jnp.einsum('mpq,qk->mkp', turned_imag, sin_two, precision=high)  9.16 us
    unnamed x1, other arithmetic  8.19 us
    dot_general x1, matrix products, to_lags(): jnp.einsum('mpq,qk->mkp', turned_real, cos_two, precision=high)  7.86 us
    all_to_all x1, waiting for transfers between devices, copy_for_each(): lax.all_to_all(jnp.broadcast_to(array[None], (peers, *array.shape)), axis...  7.57 us
    all_to_all x1, starting transfers between devices, copy_for_each(): lax.all_to_all(jnp.broadcast_to(array[None], (peers, *array.shape)), axis...  6.61 us
    dot_general x1, matrix products, to_lags(): jnp.einsum('maq,ap->mpq', imag_cube, cos_one, precision=high)  6.39 us
  transfers between devices with their start and end apart: 1, of which 1 were waited for; matrix products, arithmetic and copies ran while one was open for 0% of the time, Pallas kernels for 0%

commit v1 on v0

v1 whole, which is shorter than its diff:
```python
import math

import jax
import jax.numpy as jnp
import numpy as np
from jax import lax
from jax.experimental import pallas as pl
from jax.experimental.pallas import tpu as pltpu
from jax.sharding import PartitionSpec as P

F = 4096
L = 2048
RES = 8
SPAN = 2 * F // RES
COLS = L // RES
LANES = 128
ROWS = 16
ROOT = math.sqrt(0.5)


def tables(norm):
    bins = np.arange(SPAN)
    lag = np.arange(COLS) - COLS // 2
    angle = 2.0 * np.pi * ((bins[:, None] * lag[None, :]) % SPAN) / SPAN
    parts = np.stack([np.cos(angle), -np.sin(angle)], 0) * norm
    parts = parts.reshape(2, SPAN // LANES, LANES, COLS).transpose(1, 0, 2, 3)
    whole = parts.reshape(2 * SPAN, COLS)
    high = whole.astype(jnp.bfloat16)
    low = (whole - high.astype(np.float64)).astype(jnp.bfloat16)
    turn = 2.0 * np.pi * (np.arange(RES)[:, None] * bins[None, :]) / (2 * F)
    twiddle = np.stack([np.cos(turn), np.sin(turn)], 1).reshape(2 * RES, SPAN)
    return high, low, twiddle.astype(np.float32)


def dequantize_kernel(codes_ref, exponents_ref, values_ref):
    scale = jnp.exp2(exponents_ref[0].astype(jnp.float32)).T
    for block in range(scale.shape[1]):
        wide = jnp.broadcast_to(scale[:, block : block + 1], (scale.shape[0], LANES))
        wide = wide.astype(jnp.bfloat16)
        at = pl.ds(block * LANES, LANES)
        for part in range(2):
            values_ref[part, 0, :, at] = codes_ref[part, 0, :, at] * wide


def dequantize(spectra, exponents):
    _, segs, chans, nbin = spectra.shape
    lanes = jnp.transpose(exponents, (0, 2, 1))
    return pl.pallas_call(
        dequantize_kernel,
        grid=(segs,),
        in_specs=[
            pl.BlockSpec((2, 1, chans, nbin), lambda g: (0, g, 0, 0)),
            pl.BlockSpec((1, lanes.shape[1], chans), lambda g: (g, 0, 0)),
        ],
        out_specs=pl.BlockSpec((2, 1, chans, nbin), lambda g: (0, g, 0, 0)),
        out_shape=jax.ShapeDtypeStruct(spectra.shape, jnp.bfloat16),
        compiler_params=pltpu.CompilerParams(vmem_limit_bytes=20 << 20),
        name="dequantize",
    )(spectra, lanes)


def times_root(re, im):
    return (re - im) * ROOT, (re + im) * ROOT


def four(x):
    (ar, ai), (br, bi), (cr, ci), (dr, di) = x
    sr, si, tr, ti = ar + cr, ai + ci, ar - cr, ai - ci
    ur, ui, vr, vi = br + dr, bi + di, br - dr, bi - di
    return [(sr + ur, si + ui), (tr - vi, ti + vr), (sr - ur, si - ui), (tr + vi, ti - vr)]


def lags_kernel(base, values_ref, slab_ref, twiddle_ref, high_ref, low_ref, out_ref, hi_ref, lo_ref, acc_ref):
    chans = out_ref.shape[1]
    segs = values_ref.shape[1]
    steps = SPAN // LANES

    def produce(n, slot):
        def at(j):
            return pl.ds(pl.multiple_of(j * SPAN + n * LANES, LANES), LANES)

        for r in range(0, chans, ROWS):
            x = []
            for j in range(RES // 2):
                re = im = None
                for g in range(segs):
                    vr = values_ref[0, g, pl.ds(base + r, ROWS), at(j)].astype(jnp.float32)
                    vi = values_ref[1, g, pl.ds(base + r, ROWS), at(j)].astype(jnp.float32)
                    sr = slab_ref[pl.ds(g, 1), at(j)]
                    si = slab_ref[pl.ds(segs + g, 1), at(j)]
                    pr = sr * vr + si * vi
                    pi = sr * vi - si * vr
                    re = pr if re is None else re + pr
                    im = pi if im is None else im + pi
                x.append((re, im))
            even = four(x)
            (br, bi), (dr, di) = x[1], x[3]
            odd = four(
                [
                    x[0],
                    times_root(br, bi),
                    (-x[2][1], x[2][0]),
                    ((-dr - di) * ROOT, (dr - di) * ROOT),
                ]
            )
            for u in range(RES):
                gr, gi = even[u // 2] if u % 2 == 0 else odd[u // 2]
                if u:
                    cos = twiddle_ref[pl.ds(2 * u, 1), at(0)]
                    sin = twiddle_ref[pl.ds(2 * u + 1, 1), at(0)]
                    gr, gi = gr * cos - gi * sin, gr * sin + gi * cos
                for k, part in enumerate((gr, gi)):
                    top = part.astype(jnp.bfloat16)
                    rest = (part - top.astype(jnp.float32)).astype(jnp.bfloat16)
                    where = (slot, pl.ds(u * chans + r, ROWS), pl.ds(k * LANES, LANES))
                    hi_ref[where] = top
                    lo_ref[where] = rest

    def contract(n, slot):
        rows = pl.ds(pl.multiple_of(n * 2 * LANES, 2 * LANES), 2 * LANES)
        whi = high_ref[rows, :]
        hi = hi_ref[slot]
        dot = lambda a, b: jnp.dot(a, b, preferred_element_type=jnp.float32)
        return dot(hi, whi) + dot(lo_ref[slot], whi) + dot(hi, low_ref[rows, :])

    produce(0, 0)
    acc_ref[...] = jnp.zeros_like(acc_ref)

    def step(n, carry):
        produce(n, n % 2)
        acc_ref[...] += contract(n - 1, (n - 1) % 2)
        return carry

    lax.fori_loop(1, steps, step, 0)
    acc_ref[...] += contract(steps - 1, (steps - 1) % 2)

    piece = COLS // RES
    per = LANES // piece
    lane = lax.broadcasted_iota(jnp.int32, (8, LANES), 1)
    for r in range(0, chans, 8):
        turned = []
        for u in range(RES):
            halves = [acc_ref[pl.ds(u * chans + r, 8), pl.ds(h * LANES, LANES)] for h in range(2)]
            shift = piece * u
            if shift >= LANES:
                halves = halves[::-1]
                shift -= LANES
            if shift:
                a, b = (pltpu.roll(x, shift, 1) for x in halves)
                head = lane < shift
                halves = [jnp.where(head, b, a), jnp.where(head, a, b)]
            turned.append(halves)
        for w in range(RES):
            for h in range(2):
                picks = [turned[(h * per + s - w) % RES][h] for s in range(per)]
                left = jnp.where(lane < piece, picks[0], picks[1])
                right = jnp.where(lane < 3 * piece, picks[2], picks[3])
                out_ref[w, pl.ds(r, 8), pl.ds(h * LANES, LANES)] = jnp.where(lane < 2 * piece, left, right)


def partial_lags(values, slab, tabs, base, chans):
    high, low, twiddle = tabs
    vmem = pl.BlockSpec(memory_space=pltpu.VMEM)
    return pl.pallas_call(
        lambda *refs: lags_kernel(base, *refs),
        in_specs=[vmem] * 5,
        out_specs=vmem,
        out_shape=jax.ShapeDtypeStruct((RES, chans, COLS), jnp.float32),
        scratch_shapes=[
            pltpu.VMEM((2, RES * chans, 2 * LANES), jnp.bfloat16),
            pltpu.VMEM((2, RES * chans, 2 * LANES), jnp.bfloat16),
            pltpu.VMEM((RES * chans, COLS), jnp.float32),
        ],
        compiler_params=pltpu.CompilerParams(vmem_limit_bytes=16 << 20),
        name="lags",
    )(values, slab, twiddle, high, low)


def finish_kernel(own_ref, tiles_ref, out_ref):
    total = tiles_ref[0]
    for peer in range(1, tiles_ref.shape[0]):
        total = total + tiles_ref[peer]
    piece = COLS // RES
    place = lax.broadcasted_iota(jnp.int32, (COLS, COLS), 0)
    lag = lax.broadcasted_iota(jnp.int32, (COLS, COLS), 1)
    residue = (place // piece - own_ref[0] + RES) % RES
    order = jnp.where(lag == place % piece * RES + residue, 1.0, 0.0).astype(jnp.bfloat16)
    first = total.astype(jnp.bfloat16)
    rest = total - first.astype(jnp.float32)
    second = rest.astype(jnp.bfloat16)
    third = (rest - second.astype(jnp.float32)).astype(jnp.bfloat16)
    dot = lambda a: jnp.dot(a, order, preferred_element_type=jnp.float32)
    out_ref[...] = (dot(third) + dot(second)) + dot(first)


def finish(own, tiles):
    return pl.pallas_call(
        finish_kernel,
        in_specs=[pl.BlockSpec(memory_space=pltpu.SMEM), pl.BlockSpec(memory_space=pltpu.VMEM)],
        out_specs=pl.BlockSpec(memory_space=pltpu.VMEM),
        out_shape=jax.ShapeDtypeStruct(tiles.shape[1:], jnp.float32),
        compiler_params=pltpu.CompilerParams(vmem_limit_bytes=8 << 20),
        name="finish",
    )(own, tiles)


def own_slab(spectra, exponents, source_channels):
    local_count = spectra.shape[2]
    local_index = source_channels[0] - lax.axis_index("chan") * local_count
    owned = (local_index >= 0) & (local_index < local_count)
    clipped = jnp.clip(local_index, 0, local_count - 1)
    codes = lax.dynamic_index_in_dim(spectra, clipped, 2, keepdims=False).astype(jnp.float32)
    scale = jnp.exp2(lax.dynamic_index_in_dim(exponents, clipped, 1, keepdims=False).astype(jnp.float32))
    scale = jnp.where(owned, scale, 0.0)
    block = spectra.shape[3] // exponents.shape[2]
    return codes * jnp.repeat(scale, block, axis=1)[None]


def spread(slab):
    peers = lax.axis_size("chan")
    tiles = lax.all_to_all(slab.reshape(peers, -1), "chan", 0, 0, tiled=True)
    own = jnp.sum(tiles, axis=0)
    whole = lax.all_to_all(jnp.broadcast_to(own[None], (peers, own.shape[0])), "chan", 0, 0, tiled=True)
    return whole.reshape(4, -1)


def body(spectra, exponents, source_channels):
    chans = spectra.shape[2]
    segs = spectra.shape[1] * lax.axis_size("win")
    slab = spread(own_slab(spectra, exponents, source_channels))
    values = dequantize(spectra, exponents)
    tabs = tables(1.0 / math.sqrt(4.0 * F * segs))
    partial = partial_lags(values, slab, tabs, 0, chans)
    tiles = lax.all_to_all(partial, "win", 0, 0, tiled=True)
    own = lax.axis_index("win").reshape(1).astype(jnp.int32)
    return finish(own, tiles)[None]


def solution(mesh):
    return jax.shard_map(
        body,
        mesh=mesh,
        in_specs=(P(None, "win", "chan", None), P("win", "chan", None), P()),
        out_specs=P(None, "chan", "win"),
        check_vma=False,
    )
```

time: 170 us -> 71.3 us (0.42)
  matrix products: 48.4 us -> 0 us
  local copies, waits for them, and re-layouts: 46.5 us -> 8.08 us
  blocking collectives: 39.9 us -> 19.2 us
  other arithmetic: 18.2 us -> 2.35 us
  Pallas kernels: 0 us -> 11.3 us
  waiting for transfers between devices: 7.57 us -> 16.7 us
  starting transfers between devices: 6.61 us -> 11.7 us
    dot_general x6 -> x0, matrix products: 48.4 us -> none  [the longest x1 13.3 us: to_lags(): jnp.einsum('maq,ap->mpq', imag_cube, sin_one, precision=high)]
    all_to_all x2 -> x1, blocking collectives: 39.9 us -> 19.2 us  [spread(): tiles = lax.all_to_all(slab.reshape(peers, -1), 'chan', 0, 0, tiled=True)]
    pallas_call x0 -> x3, Pallas kernels: none -> 11.3 us  [the longest x1 8.48 us: partial_lags(): pl.pallas_call(lambda *refs: lags_kernel(base, *refs), in_specs=[vmem] *...]
    dot_general x4 -> x0, local copies, waits for them, and re-layouts: 10.7 us -> none  [the longest x1 2.94 us: body(): jnp.einsum('gsf,gcf->scf', slab[1], values[1], precision=high)]
    reshape x3 -> x1, local copies, waits for them, and re-layouts: 9.32 us -> 0.05 us  [spread(): return whole.reshape(4, -1)]
    all_to_all x1 -> x2, waiting for transfers between devices: 7.57 us -> 16.7 us  [the longest x1 15.7 us: body(): tiles = lax.all_to_all(partial, 'win', 0, 0, tiled=True)]
    unnamed x1 -> x0, other arithmetic: 8.19 us -> none
    sub x1 -> x0, local copies, waits for them, and re-layouts: 5.48 us -> none  [to_lags(): section_real * twiddle_cos[None] - section_imag * twiddle_sin[None]]
  transfers between devices with their start and end apart: 1 -> 2, of which waited for: 1 -> 2; matrix products, arithmetic and copies ran while one was open for 0% -> 0% of each run, Pallas kernels for 0% -> 3%
where the time goes in v1:
time: 71.3 us; the launch traced here: 70.1 us
  blocking collectives  19.2 us (27%)
  waiting for transfers between devices  16.7 us (23%)
  starting transfers between devices  11.7 us (16%)
  Pallas kernels  11.3 us (16%)
  local copies, waits for them, and re-layouts  8.08 us (11%)
  other arithmetic  2.35 us (3%)
  between operations  0.79 us (1%)
    all_to_all x1, blocking collectives, spread(): tiles = lax.all_to_all(slab.reshape(peers, -1), 'chan', 0, 0, tiled=True)  19.2 us
    all_to_all x1, waiting for transfers between devices, body(): tiles = lax.all_to_all(partial, 'win', 0, 0, tiled=True)  15.7 us
    pallas_call x1, Pallas kernels, partial_lags(): pl.pallas_call(lambda *refs: lags_kernel(base, *refs), in_specs=[vmem] *...  8.48 us
    unnamed x16, local copies, waits for them, and re-layouts  7.16 us
    all_to_all x1, starting transfers between devices, spread(): lax.all_to_all(jnp.broadcast_to(own[None], (peers, own.shape[0])), 'chan'...  6.61 us
    all_to_all x1, starting transfers between devices, body(): tiles = lax.all_to_all(partial, 'win', 0, 0, tiled=True)  5.1 us
    pallas_call x1, Pallas kernels, dequantize(): pl.pallas_call(dequantize_kernel, grid=(segs,), in_specs=[pl.BlockSpec((2...  1.82 us
  transfers between devices with their start and end apart: 2, of which 2 were waited for; matrix products, arithmetic and copies ran while one was open for 0% of the time, Pallas kernels for 3%

profile of v1, /device:TPU:4, one launch (start us, length us, event | category | flops | bytes accessed | tf_op | source)
XLA Modules:
  0.0 70.1 jit_solution(10399855851315449212)
XLA Ops:
  0.7 0.9 %select_reduce_fusion = f32[2,32]{1,0:T(2,128)S(1)} fusion(s32[2,128,32]{1,2,0:T(8,128)} %param.7, s32[]{:T(128)S(6)} %min.4, pred[]{:T(512)S(6)} %and.5), kind=kLoop, calls=%fused_computation.2 | loop fusion | flops 192 | bytes 517 | tf_op jit(solution)/shard_map/jit(_where)/select_n | solution.py:214
  1.6 0.1 broadcast_bitcast_fusion
  1.7 0.1 mul.26
  1.8 1.2 %convert_reduce_fusion = f32[2,2,4096]{2,1,0:T(2,128)S(1)} fusion(bf16[2,2,128,4096]{3,2,1,0:T(8,128)(2,1)} %codes_ref.1, s32[]{:T(128)S(6)} %min.4), kind=kLoop, calls=%fused_computation | loop fusion | flops 16384 | bytes 98308 | tf_op jit(solution)/shard_map/convert_element_type | solution.py:212
  3.0 0.1 reshape.50
  3.1 0.1 copy.7
  3.2 19.2 %all_to_all.17 = f32[32,1,512]{2,1,0:T(1,128)S(1)} all-to-all(f32[32,1,512]{2,1,0:T(1,128)S(1)} %copy.7), channel_id=1, replica_groups=mesh['chan'=32,'win'=8] {'chan'}, dimensions={0} | all-to-all | bytes 131072 | tf_op jit(solution)/shard_map/all_to_all | solution.py:221
  22.3 0.1 reduce_sum.9
  22.4 0.7 broadcast_in_dim.18
  23.1 6.6 %all-to-all-start.1 = ((f32[32,1,512]{2,1,0:T(1,128)}), f32[32,1,512]{2,1,0:T(1,128)S(1)}, u32[]{:S(2)}, u32[]{:S(2)}) async-start(f32[32,1,512]{2,1,0:T(1,128)} %broadcast_in_dim.18), calls=%async_computation.1 | async-start | bytes 131072 | tf_op jit(solution)/shard_map/all_to_all | solution.py:223
  29.7 0.0 copy-start.2
  29.7 2.2 %copy-done.2 = bf16[2,2,128,4096]{3,2,1,0:T(8,128)(2,1)S(1)} copy-done((bf16[2,2,128,4096]{3,2,1,0:T(8,128)(2,1)S(1)}, bf16[2,2,128,4096]{3,2,1,0:T(8,128)(2,1)}, u32[]{:S(2)}) %copy-start.2) | copy-done | bytes 4194328
  31.9 0.0 copy-start.5
  31.9 0.8 %copy-done.5 = s32[2,128,32]{1,2,0:T(8,128)S(1)} copy-done((s32[2,128,32]{1,2,0:T(8,128)S(1)}, s32[2,128,32]{1,2,0:T(8,128)}, u32[]{:S(2)}) %copy-start.5) | copy-done | bytes 32792
  32.6 0.0 copy-start.3
  32.6 0.0 copy-start.4
  32.6 0.0 copy-start.6
  32.6 1.8 %dequantize.1.refs_0_ = bf16[2,2,128,4096]{3,2,1,0:T(8,128)(2,1)S(1)} custom-call(bf16[2,2,128,4096]{3,2,1,0:T(8,128)(2,1)S(1)} %copy-done.2, s32[2,32,128]{2,1,0:T(8,128)S(1)} %bitcast.10), custom_call_target="tpu_custom_call" | custom-call | tf_op jit(solution)/shard_map/dequantize/pallas_call | solution.py:48
  34.5 0.0 copy-start
  34.5 1.9 %copy-done = bf16[2,2,128,4096]{3,2,1,0:T(8,128)(2,1)} copy-done((bf16[2,2,128,4096]{3,2,1,0:T(8,128)(2,1)}, bf16[2,2,128,4096]{3,2,1,0:T(8,128)(2,1)S(1)}, u32[]{:S(2)}) %copy-start) | copy-done | bytes 4194328
  36.4 1.0 %all-to-all-done.1 = f32[32,1,512]{2,1,0:T(1,128)S(1)} async-done(((f32[32,1,512]{2,1,0:T(1,128)}), f32[32,1,512]{2,1,0:T(1,128)S(1)}, u32[]{:S(2)}, u32[]{:S(2)}) %all-to-all-start.1) | async-done | bytes 65568 | tf_op jit(solution)/shard_map/all_to_all | solution.py:223
  37.4 0.2 reduce.3
  37.6 0.0 copy-done.3
  37.6 0.0 copy-done.4
  37.6 0.0 copy-done.6
  37.6 0.0 copy-start.1
  37.7 2.2 %copy-done.1 = bf16[2,2,128,4096]{3,2,1,0:T(8,128)(2,1)S(1)} copy-done((bf16[2,2,128,4096]{3,2,1,0:T(8,128)(2,1)S(1)}, bf16[2,2,128,4096]{3,2,1,0:T(8,128)(2,1)}, u32[]{:S(2)}) %copy-start.1) | copy-done | bytes 4194328
  39.8 8.5 %lags.1 = f32[8,128,256]{2,1,0:T(8,128)} custom-call(bf16[2,2,128,4096]{3,2,1,0:T(8,128)(2,1)S(1)} %copy-done.1, f32[4,4096]{1,0:T(4,128)S(1)} %reshape.49.refs_1_, f32[16,1024]{1,0:T(8,128)S(1)} %copy-done.6, bf16[2048,256]{1,0:T(8,128)(2,1)S(1)} %copy-done.4, bf16[2048,256]{1,0:T(8,128)(2,1)S(1)} %copy-done.3), custom_call_target="tpu_custom_call" | custom-call | tf_op jit(solution)/shard_map/lags/pallas_call | solution.py:164
  48.3 5.1 %all-to-all-start.2 = ((f32[8,128,256]{2,1,0:T(8,128)}), f32[8,128,256]{2,1,0:T(8,128)S(1)}, u32[]{:S(2)}, u32[]{:S(2)}) async-start(f32[8,128,256]{2,1,0:T(8,128)} %lags.1), calls=%async_computation.2 | async-start | bytes 2097152 | tf_op jit(solution)/shard_map/all_to_all | solution.py:234
  53.4 15.7 %all-to-all-done.2.tiles_ref = f32[8,128,256]{2,1,0:T(8,128)S(1)} async-done(((f32[8,128,256]{2,1,0:T(8,128)}), f32[8,128,256]{2,1,0:T(8,128)S(1)}, u32[]{:S(2)}, u32[]{:S(2)}) %all-to-all-start.2) | async-done | bytes 1048608 | tf_op jit(solution)/shard_map/all_to_all | solution.py:234
  69.1 0.9 %finish.1 = f32[128,256]{1,0:T(8,128)} custom-call(s32[1]{0:T(128)} %bitcast.own_ref, f32[8,128,256]{2,1,0:T(8,128)S(1)} %all-to-all-done.2.tiles_ref), custom_call_target="tpu_custom_call" | custom-call | tf_op jit(solution)/shard_map/finish/pallas_call | solution.py:197
  (4 shorter events, 0.1 us)
Async XLA Ops:
  23.1 14.3 %all-to-all-start.1 = ((f32[32,1,512]{2,1,0:T(1,128)}), f32[32,1,512]{2,1,0:T(1,128)S(1)}, u32[]{:S(2)}, u32[]{:S(2)}) async-start(f32[32,1,512]{2,1,0:T(1,128)} %broadcast_in_dim.18), calls=%async_computation.1 | async-start | bytes 131072 | tf_op jit(solution)/shard_map/all_to_all | solution.py:223
  29.7 2.2 %copy-start.2 = (bf16[2,2,128,4096]{3,2,1,0:T(8,128)(2,1)S(1)}, bf16[2,2,128,4096]{3,2,1,0:T(8,128)(2,1)}, u32[]{:S(2)}) copy-start(bf16[2,2,128,4096]{3,2,1,0:T(8,128)(2,1)} %codes_ref.1) | copy-start | bytes 12582916
  31.9 0.8 %copy-start.5 = (s32[2,128,32]{1,2,0:T(8,128)S(1)}, s32[2,128,32]{1,2,0:T(8,128)}, u32[]{:S(2)}) copy-start(s32[2,128,32]{1,2,0:T(8,128)} %param.7) | copy-start | bytes 98308
  32.6 5.0 %copy-start.3 = (bf16[2048,256]{1,0:T(8,128)(2,1)S(1)}, bf16[2048,256]{1,0:T(8,128)(2,1)}, u32[]{:S(2)}) copy-start(bf16[2048,256]{1,0:T(8,128)(2,1)} %constant.36.clone.refs_4_) | copy-start | bytes 3145732
  32.6 5.0 %copy-start.4 = (bf16[2048,256]{1,0:T(8,128)(2,1)S(1)}, bf16[2048,256]{1,0:T(8,128)(2,1)}, u32[]{:S(2)}) copy-start(bf16[2048,256]{1,0:T(8,128)(2,1)} %constant.35.clone.refs_3_) | copy-start | bytes 3145732
  32.6 5.0 %copy-start.6 = (f32[16,1024]{1,0:T(8,128)S(1)}, f32[16,1024]{1,0:T(8,128)}, u32[]{:S(2)}) copy-start(f32[16,1024]{1,0:T(8,128)} %constant.34.clone.refs_2_) | copy-start | bytes 196612
  34.5 1.9 %copy-start = (bf16[2,2,128,4096]{3,2,1,0:T(8,128)(2,1)}, bf16[2,2,128,4096]{3,2,1,0:T(8,128)(2,1)S(1)}, u32[]{:S(2)}) copy-start(bf16[2,2,128,4096]{3,2,1,0:T(8,128)(2,1)S(1)} %dequantize.1.refs_0_) | copy-start | bytes 12582916
  37.6 2.2 %copy-start.1 = (bf16[2,2,128,4096]{3,2,1,0:T(8,128)(2,1)S(1)}, bf16[2,2,128,4096]{3,2,1,0:T(8,128)(2,1)}, u32[]{:S(2)}) copy-start(bf16[2,2,128,4096]{3,2,1,0:T(8,128)(2,1)} %copy-done) | copy-start | bytes 12582916
  48.3 20.8 %all-to-all-start.2 = ((f32[8,128,256]{2,1,0:T(8,128)}), f32[8,128,256]{2,1,0:T(8,128)S(1)}, u32[]{:S(2)}, u32[]{:S(2)}) async-start(f32[8,128,256]{2,1,0:T(8,128)} %lags.1), calls=%async_computation.2 | async-start | bytes 2097152 | tf_op jit(solution)/shard_map/all_to_all | solution.py:234

commit v2 on v1

--- a/solution.py
+++ b/solution.py
@@ -33,18 +33,18 @@
 
 
 def dequantize_kernel(codes_ref, exponents_ref, values_ref):
+    seg = pl.program_id(0)
     scale = jnp.exp2(exponents_ref[0].astype(jnp.float32)).T
     for block in range(scale.shape[1]):
         wide = jnp.broadcast_to(scale[:, block : block + 1], (scale.shape[0], LANES))
         wide = wide.astype(jnp.bfloat16)
         at = pl.ds(block * LANES, LANES)
         for part in range(2):
-            values_ref[part, 0, :, at] = codes_ref[part, 0, :, at] * wide
-
-
-def dequantize(spectra, exponents):
+            values_ref[part, seg, :, at] = codes_ref[part, 0, :, at] * wide
+
+
+def dequantize(spectra, lanes):
     _, segs, chans, nbin = spectra.shape
-    lanes = jnp.transpose(exponents, (0, 2, 1))
     return pl.pallas_call(
         dequantize_kernel,
         grid=(segs,),
@@ -52,11 +52,56 @@
             pl.BlockSpec((2, 1, chans, nbin), lambda g: (0, g, 0, 0)),
             pl.BlockSpec((1, lanes.shape[1], chans), lambda g: (g, 0, 0)),
         ],
-        out_specs=pl.BlockSpec((2, 1, chans, nbin), lambda g: (0, g, 0, 0)),
+        out_specs=pl.BlockSpec(memory_space=pltpu.VMEM),
         out_shape=jax.ShapeDtypeStruct(spectra.shape, jnp.bfloat16),
         compiler_params=pltpu.CompilerParams(vmem_limit_bytes=20 << 20),
         name="dequantize",
     )(spectra, lanes)
+
+
+def pick_kernel(local_ref, codes_ref, exponents_ref, slab_ref, rows_ref, lanes_ref, row_sem, lane_sem):
+    segs, blocks, chans = lanes_ref.shape
+    local = local_ref[0]
+    owned = (local >= 0) & (local < chans)
+    row = jnp.clip(local, 0, chans - 1)
+    first = pl.multiple_of(row // ROWS * ROWS, ROWS)
+    rows_in = pltpu.make_async_copy(codes_ref.at[:, :, pl.ds(first, ROWS), :], rows_ref, row_sem)
+    lanes_in = pltpu.make_async_copy(exponents_ref, lanes_ref, lane_sem)
+    rows_in.start()
+    lanes_in.start()
+    own_lane = lax.broadcasted_iota(jnp.int32, (blocks, chans), 1) == row
+    own_row = lax.broadcasted_iota(jnp.int32, (ROWS, LANES), 0) == row % ROWS
+    lanes_in.wait()
+    rows_in.wait()
+    for g in range(segs):
+        exponent = jnp.sum(jnp.where(own_lane, lanes_ref[g].astype(jnp.float32), 0.0), axis=1, keepdims=True)
+        scale = jnp.where(owned, jnp.exp2(exponent), 0.0)
+        scale = jnp.broadcast_to(scale, (blocks, LANES)).astype(jnp.bfloat16).astype(jnp.float32)
+        for part in range(2):
+            for block in range(blocks):
+                at = pl.ds(block * LANES, LANES)
+                codes = rows_ref[part, g, :, at].astype(jnp.float32)
+                code = jnp.sum(jnp.where(own_row, codes, 0.0), axis=0, keepdims=True)
+                slab_ref[pl.ds(part * segs + g, 1), at] = code * scale[block : block + 1]
+
+
+def pick(local, spectra, lanes):
+    _, segs, _, nbin = spectra.shape
+    hbm = pl.BlockSpec(memory_space=pltpu.MemorySpace.HBM)
+    return pl.pallas_call(
+        pick_kernel,
+        in_specs=[pl.BlockSpec(memory_space=pltpu.SMEM), hbm, hbm],
+        out_specs=pl.BlockSpec(memory_space=pltpu.VMEM),
+        out_shape=jax.ShapeDtypeStruct((2 * segs, nbin), jnp.float32),
+        scratch_shapes=[
+            pltpu.VMEM((2, segs, ROWS, nbin), jnp.bfloat16),
+            pltpu.VMEM(lanes.shape, jnp.int32),
+            pltpu.SemaphoreType.DMA(()),
+            pltpu.SemaphoreType.DMA(()),
+        ],
+        compiler_params=pltpu.CompilerParams(vmem_limit_bytes=4 << 20),
+        name="pick",
+    )(local, spectra, lanes)
 
 
 def times_root(re, im):
@@ -204,31 +249,22 @@
     )(own, tiles)
 
 
-def own_slab(spectra, exponents, source_channels):
-    local_count = spectra.shape[2]
-    local_index = source_channels[0] - lax.axis_index("chan") * local_count
-    owned = (local_index >= 0) & (local_index < local_count)
-    clipped = jnp.clip(local_index, 0, local_count - 1)
-    codes = lax.dynamic_index_in_dim(spectra, clipped, 2, keepdims=False).astype(jnp.float32)
-    scale = jnp.exp2(lax.dynamic_index_in_dim(exponents, clipped, 1, keepdims=False).astype(jnp.float32))
-    scale = jnp.where(owned, scale, 0.0)
-    block = spectra.shape[3] // exponents.shape[2]
-    return codes * jnp.repeat(scale, block, axis=1)[None]
-
-
 def spread(slab):
     peers = lax.axis_size("chan")
-    tiles = lax.all_to_all(slab.reshape(peers, -1), "chan", 0, 0, tiled=True)
-    own = jnp.sum(tiles, axis=0)
-    whole = lax.all_to_all(jnp.broadcast_to(own[None], (peers, own.shape[0])), "chan", 0, 0, tiled=True)
-    return whole.reshape(4, -1)
+    for bit in (1, 16, 2, 4, 8):
+        slab = slab + lax.ppermute(slab, "chan", [(peer, peer ^ bit) for peer in range(peers)])
+    return slab
 
 
 def body(spectra, exponents, source_channels):
     chans = spectra.shape[2]
     segs = spectra.shape[1] * lax.axis_size("win")
-    slab = spread(own_slab(spectra, exponents, source_channels))
-    values = dequantize(spectra, exponents)
+    stay = lambda array: pltpu.with_memory_space_constraint(array, pltpu.MemorySpace.HBM)
+    spectra = stay(spectra)
+    lanes = stay(jnp.transpose(exponents, (0, 2, 1)))
+    local = source_channels - lax.axis_index("chan") * chans
+    slab = spread(pick(local, spectra, lanes))
+    values = dequantize(spectra, lanes)
     tabs = tables(1.0 / math.sqrt(4.0 * F * segs))
     partial = partial_lags(values, slab, tabs, 0, chans)
     tiles = lax.all_to_all(partial, "win", 0, 0, tiled=True)

time: 71.3 us -> 56.9 us (0.80); the launches traced: 70.1 us -> 56.8 us
  blocking collectives: 19.2 us -> 0 us
  starting transfers between devices: 11.7 us -> 20.5 us
  local copies, waits for them, and re-layouts: 8.08 us -> 0.02 us
  waiting for transfers between devices: 16.7 us -> 21.8 us
  Pallas kernels: 11.3 us -> 13.6 us
  other arithmetic: 2.35 us -> 0.09 us
    all_to_all x1 -> x0, blocking collectives: 19.2 us -> none  [spread(): tiles = lax.all_to_all(slab.reshape(peers, -1), 'chan', 0, 0, tiled=True)]
    ppermute x0 -> x5, starting transfers between devices: none -> 15.4 us  [spread(): lax.ppermute(slab, 'chan', [(peer, peer ^ bit) for peer in range(peers)])]
    ppermute x0 -> x5, waiting for transfers between devices: none -> 9.39 us  [spread(): lax.ppermute(slab, 'chan', [(peer, peer ^ bit) for peer in range(peers)])]
    unnamed x16 -> x6, local copies, waits for them, and re-layouts: 7.16 us -> 0.02 us
    all_to_all x1 -> x0, starting transfers between devices: 6.61 us -> none  [spread(): lax.all_to_all(jnp.broadcast_to(own[None], (peers, own.shape[0])), 'chan'...]
    all_to_all x1, waiting for transfers between devices: 15.7 us -> 12.4 us  [body(): tiles = lax.all_to_all(partial, 'win', 0, 0, tiled=True)]
    pallas_call x0 -> x1, Pallas kernels: none -> 1.33 us  [pick(): pl.pallas_call(pick_kernel, in_specs=[pl.BlockSpec(memory_space=pltpu.SME...]
    convert_element_type x1 -> x0, other arithmetic: 1.18 us -> none  [own_slab(): lax.dynamic_index_in_dim(spectra, clipped, 2, keepdims=False)]
  transfers between devices with their start and end apart: 2 -> 6, of which waited for: 2 -> 5; matrix products, arithmetic and copies ran while one was open for 0% -> 0% of each run, Pallas kernels for 3% -> 5%
where the time goes in v2:
time: 56.9 us; the launch traced here: 56.8 us
  waiting for transfers between devices  21.8 us (38%)
  starting transfers between devices  20.5 us (36%)
  Pallas kernels  13.6 us (24%)
  between operations  0.76 us (1%)
    ppermute x5, starting transfers between devices, spread(): lax.ppermute(slab, 'chan', [(peer, peer ^ bit) for peer in range(peers)])  15.4 us
    all_to_all x1, waiting for transfers between devices, body(): tiles = lax.all_to_all(partial, 'win', 0, 0, tiled=True)  12.4 us
    ppermute x5, waiting for transfers between devices, spread(): lax.ppermute(slab, 'chan', [(peer, peer ^ bit) for peer in range(peers)])  9.39 us
    pallas_call x1, Pallas kernels, partial_lags(): pl.pallas_call(lambda *refs: lags_kernel(base, *refs), in_specs=[vmem] *...  8.46 us
    all_to_all x1, starting transfers between devices, body(): tiles = lax.all_to_all(partial, 'win', 0, 0, tiled=True)  5.1 us
    pallas_call x1, Pallas kernels, dequantize(): pl.pallas_call(dequantize_kernel, grid=(segs,), in_specs=[pl.BlockSpec((2...  2.87 us
    pallas_call x1, Pallas kernels, pick(): pl.pallas_call(pick_kernel, in_specs=[pl.BlockSpec(memory_space=pltpu.SME...  1.33 us
  transfers between devices with their start and end apart: 6, of which 5 were waited for; matrix products, arithmetic and copies ran while one was open for 0% of the time, Pallas kernels for 5%

profile of v2, /device:TPU:4, one launch (start us, length us, event | category | flops | bytes accessed | tf_op | source)
XLA Modules:
  0.0 56.8 jit_solution(17625733164124680380)
XLA Ops:
  0.7 1.3 %pick.1 = f32[4,4096]{1,0:T(4,128)S(1)} custom-call(s32[1]{0:T(128)S(6)} %sub.7.local_ref, bf16[2,2,128,4096]{3,2,1,0:T(8,128)(2,1)} %codes_ref.3, s32[2,32,128]{2,1,0:T(8,128)} %bitcast.4), custom_call_target="tpu_custom_call" | custom-call | tf_op jit(solution)/shard_map/pick/pallas_call | solution.py:91
  2.0 0.1 collective-permute-start
  2.1 1.2 %collective-permute-done = f32[4,4096]{1,0:T(4,128)S(1)} collective-permute-done((f32[4,4096]{1,0:T(4,128)S(1)}, f32[4,4096]{1,0:T(4,128)S(1)}, u32[]{:S(2)}, u32[]{:S(2)}) %collective-permute-start) | collective-permute-done | bytes 65568 | tf_op jit(solution)/shard_map/ppermute | solution.py:255
  3.4 2.3 %collective-permute-start.1 = (f32[4,4096]{1,0:T(4,128)S(1)}, f32[4,4096]{1,0:T(4,128)S(1)}, u32[]{:S(2)}, u32[]{:S(2)}) collective-permute-start(f32[4,4096]{1,0:T(4,128)S(1)} %add.15), channel_id=1, source_target_pairs={{0,128},{8,136},{16,144},{24,152},{32,160},{40,168},{48,176},{56,1... | collective-permute-start | bytes 196616 | tf_op jit(solution)/shard_map/ppermute | solution.py:255
  5.7 3.6 %collective-permute-done.1 = f32[4,4096]{1,0:T(4,128)S(1)} collective-permute-done((f32[4,4096]{1,0:T(4,128)S(1)}, f32[4,4096]{1,0:T(4,128)S(1)}, u32[]{:S(2)}, u32[]{:S(2)}) %collective-permute-start.1) | collective-permute-done | bytes 65568 | tf_op jit(solution)/shard_map/ppermute | solution.py:255
  9.2 2.0 %collective-permute-start.2 = (f32[4,4096]{1,0:T(4,128)S(1)}, f32[4,4096]{1,0:T(4,128)S(1)}, u32[]{:S(2)}, u32[]{:S(2)}) collective-permute-start(f32[4,4096]{1,0:T(4,128)S(1)} %add.16), channel_id=1, source_target_pairs={{0,16},{8,24},{16,0},{24,8},{32,48},{40,56},{48,32},{56,40},{64,80... | collective-permute-start | bytes 196616 | tf_op jit(solution)/shard_map/ppermute | solution.py:255
  11.2 2.3 %collective-permute-done.2 = f32[4,4096]{1,0:T(4,128)S(1)} collective-permute-done((f32[4,4096]{1,0:T(4,128)S(1)}, f32[4,4096]{1,0:T(4,128)S(1)}, u32[]{:S(2)}, u32[]{:S(2)}) %collective-permute-start.2) | collective-permute-done | bytes 65568 | tf_op jit(solution)/shard_map/ppermute | solution.py:255
  13.6 3.4 %collective-permute-start.3 = (f32[4,4096]{1,0:T(4,128)S(1)}, f32[4,4096]{1,0:T(4,128)S(1)}, u32[]{:S(2)}, u32[]{:S(2)}) collective-permute-start(f32[4,4096]{1,0:T(4,128)S(1)} %add.17), channel_id=1, source_target_pairs={{0,32},{8,40},{16,48},{24,56},{32,0},{40,8},{48,16},{56,24},{64,96... | collective-permute-start | bytes 196616 | tf_op jit(solution)/shard_map/ppermute | solution.py:255
  17.0 2.2 %collective-permute-done.3 = f32[4,4096]{1,0:T(4,128)S(1)} collective-permute-done((f32[4,4096]{1,0:T(4,128)S(1)}, f32[4,4096]{1,0:T(4,128)S(1)}, u32[]{:S(2)}, u32[]{:S(2)}) %collective-permute-start.3) | collective-permute-done | bytes 65568 | tf_op jit(solution)/shard_map/ppermute | solution.py:255
  19.2 0.0 copy-start
  19.2 0.0 copy-start.1
  19.3 0.0 copy-start.2
  19.3 7.6 %collective-permute-start.4 = (f32[4,4096]{1,0:T(4,128)S(1)}, f32[4,4096]{1,0:T(4,128)S(1)}, u32[]{:S(2)}, u32[]{:S(2)}) collective-permute-start(f32[4,4096]{1,0:T(4,128)S(1)} %add.18), channel_id=1, source_target_pairs={{0,64},{8,72},{16,80},{24,88},{32,96},{40,104},{48,112},{56,120},{... | collective-permute-start | bytes 196616 | tf_op jit(solution)/shard_map/ppermute | solution.py:255
  26.9 2.9 %dequantize.1.refs_0_ = bf16[2,2,128,4096]{3,2,1,0:T(8,128)(2,1)S(1)} custom-call(bf16[2,2,128,4096]{3,2,1,0:T(8,128)(2,1)} %codes_ref.3, s32[2,32,128]{2,1,0:T(8,128)} %bitcast.5), custom_call_target="tpu_custom_call" | custom-call | tf_op jit(solution)/shard_map/dequantize/pallas_call | solution.py:48
  29.8 0.0 collective-permute-done.4
  29.8 0.0 copy-done
  29.8 0.0 copy-done.1
  29.8 0.0 copy-done.2
  29.9 8.5 %lags.1 = f32[8,128,256]{2,1,0:T(8,128)} custom-call(bf16[2,2,128,4096]{3,2,1,0:T(8,128)(2,1)S(1)} %dequantize.1.refs_0_, f32[4,4096]{1,0:T(4,128)S(1)} %add.19.refs_1_, f32[16,1024]{1,0:T(8,128)S(1)} %copy-done.2, bf16[2048,256]{1,0:T(8,128)(2,1)S(1)} %copy-done.1, bf16[2048,256]{1,0:T(8,128)(2,1)S(1)} %copy-done), custom_call_target="tpu_custom_call" | custom-call | tf_op jit(solution)/shard_map/lags/pallas_call | solution.py:209
  38.3 5.1 %all-to-all-start = ((f32[8,128,256]{2,1,0:T(8,128)}), f32[8,128,256]{2,1,0:T(8,128)S(1)}, u32[]{:S(2)}, u32[]{:S(2)}) async-start(f32[8,128,256]{2,1,0:T(8,128)} %lags.1), calls=%async_computation | async-start | bytes 2097152 | tf_op jit(solution)/shard_map/all_to_all | solution.py:270
  43.4 12.4 %all-to-all-done.tiles_ref = f32[8,128,256]{2,1,0:T(8,128)S(1)} async-done(((f32[8,128,256]{2,1,0:T(8,128)}), f32[8,128,256]{2,1,0:T(8,128)S(1)}, u32[]{:S(2)}, u32[]{:S(2)}) %all-to-all-start) | async-done | bytes 1048608 | tf_op jit(solution)/shard_map/all_to_all | solution.py:270
  55.8 0.9 %finish.1 = f32[128,256]{1,0:T(8,128)} custom-call(s32[1]{0:T(128)} %bitcast.own_ref, f32[8,128,256]{2,1,0:T(8,128)S(1)} %all-to-all-done.tiles_ref), custom_call_target="tpu_custom_call" | custom-call | tf_op jit(solution)/shard_map/finish/pallas_call | solution.py:242
  (5 shorter events, 0.1 us)
Async XLA Ops:
  2.0 1.3 %collective-permute-start = (f32[4,4096]{1,0:T(4,128)S(1)}, f32[4,4096]{1,0:T(4,128)S(1)}, u32[]{:S(2)}, u32[]{:S(2)}) collective-permute-start(f32[4,4096]{1,0:T(4,128)S(1)} %pick.1), channel_id=1, source_target_pairs={{0,8},{8,0},{16,24},{24,16},{32,40},{40,32},{48,56},{56,48},{64,72... | collective-permute-start | bytes 196616 | tf_op jit(solution)/shard_map/ppermute | solution.py:255
  3.4 5.9 %collective-permute-start.1 = (f32[4,4096]{1,0:T(4,128)S(1)}, f32[4,4096]{1,0:T(4,128)S(1)}, u32[]{:S(2)}, u32[]{:S(2)}) collective-permute-start(f32[4,4096]{1,0:T(4,128)S(1)} %add.15), channel_id=1, source_target_pairs={{0,128},{8,136},{16,144},{24,152},{32,160},{40,168},{48,176},{56,1... | collective-permute-start | bytes 196616 | tf_op jit(solution)/shard_map/ppermute | solution.py:255
  9.2 4.4 %collective-permute-start.2 = (f32[4,4096]{1,0:T(4,128)S(1)}, f32[4,4096]{1,0:T(4,128)S(1)}, u32[]{:S(2)}, u32[]{:S(2)}) collective-permute-start(f32[4,4096]{1,0:T(4,128)S(1)} %add.16), channel_id=1, source_target_pairs={{0,16},{8,24},{16,0},{24,8},{32,48},{40,56},{48,32},{56,40},{64,80... | collective-permute-start | bytes 196616 | tf_op jit(solution)/shard_map/ppermute | solution.py:255
  13.6 5.6 %collective-permute-start.3 = (f32[4,4096]{1,0:T(4,128)S(1)}, f32[4,4096]{1,0:T(4,128)S(1)}, u32[]{:S(2)}, u32[]{:S(2)}) collective-permute-start(f32[4,4096]{1,0:T(4,128)S(1)} %add.17), channel_id=1, source_target_pairs={{0,32},{8,40},{16,48},{24,56},{32,0},{40,8},{48,16},{56,24},{64,96... | collective-permute-start | bytes 196616 | tf_op jit(solution)/shard_map/ppermute | solution.py:255
  19.2 10.6 %copy-start = (bf16[2048,256]{1,0:T(8,128)(2,1)S(1)}, bf16[2048,256]{1,0:T(8,128)(2,1)}, u32[]{:S(2)}) copy-start(bf16[2048,256]{1,0:T(8,128)(2,1)} %constant.19.clone.refs_4_) | copy-start | bytes 3145732
  19.2 10.6 %copy-start.1 = (bf16[2048,256]{1,0:T(8,128)(2,1)S(1)}, bf16[2048,256]{1,0:T(8,128)(2,1)}, u32[]{:S(2)}) copy-start(bf16[2048,256]{1,0:T(8,128)(2,1)} %constant.18.clone.refs_3_) | copy-start | bytes 3145732
  19.3 10.6 %copy-start.2 = (f32[16,1024]{1,0:T(8,128)S(1)}, f32[16,1024]{1,0:T(8,128)}, u32[]{:S(2)}) copy-start(f32[16,1024]{1,0:T(8,128)} %constant.17.clone.refs_2_) | copy-start | bytes 196612
  19.3 10.5 %collective-permute-start.4 = (f32[4,4096]{1,0:T(4,128)S(1)}, f32[4,4096]{1,0:T(4,128)S(1)}, u32[]{:S(2)}, u32[]{:S(2)}) collective-permute-start(f32[4,4096]{1,0:T(4,128)S(1)} %add.18), channel_id=1, source_target_pairs={{0,64},{8,72},{16,80},{24,88},{32,96},{40,104},{48,112},{56,120},{... | collective-permute-start | bytes 196616 | tf_op jit(solution)/shard_map/ppermute | solution.py:255
  38.3 17.5 %all-to-all-start = ((f32[8,128,256]{2,1,0:T(8,128)}), f32[8,128,256]{2,1,0:T(8,128)S(1)}, u32[]{:S(2)}, u32[]{:S(2)}) async-start(f32[8,128,256]{2,1,0:T(8,128)} %lags.1), calls=%async_computation | async-start | bytes 2097152 | tf_op jit(solution)/shard_map/all_to_all | solution.py:270

commit v3 on v2

--- a/solution.py
+++ b/solution.py
@@ -15,6 +15,7 @@
 COLS = L // RES
 LANES = 128
 ROWS = 16
+PIECE = 32
 ROOT = math.sqrt(0.5)
 
 
@@ -33,27 +34,26 @@
 
 
 def dequantize_kernel(codes_ref, exponents_ref, values_ref):
-    seg = pl.program_id(0)
+    seg, part = pl.program_id(0), pl.program_id(1)
     scale = jnp.exp2(exponents_ref[0].astype(jnp.float32)).T
     for block in range(scale.shape[1]):
         wide = jnp.broadcast_to(scale[:, block : block + 1], (scale.shape[0], LANES))
-        wide = wide.astype(jnp.bfloat16)
+        wide = wide.astype(jnp.bfloat16).astype(jnp.float32)
         at = pl.ds(block * LANES, LANES)
-        for part in range(2):
-            values_ref[part, seg, :, at] = codes_ref[part, 0, :, at] * wide
+        values_ref[part, seg, :, at] = codes_ref[0, 0, :, at].astype(jnp.float32) * wide
 
 
 def dequantize(spectra, lanes):
     _, segs, chans, nbin = spectra.shape
     return pl.pallas_call(
         dequantize_kernel,
-        grid=(segs,),
+        grid=(segs, 2),
         in_specs=[
-            pl.BlockSpec((2, 1, chans, nbin), lambda g: (0, g, 0, 0)),
-            pl.BlockSpec((1, lanes.shape[1], chans), lambda g: (g, 0, 0)),
+            pl.BlockSpec((1, 1, chans, nbin), lambda g, p: (p, g, 0, 0)),
+            pl.BlockSpec((1, lanes.shape[1], chans), lambda g, p: (g, 0, 0)),
         ],
         out_specs=pl.BlockSpec(memory_space=pltpu.VMEM),
-        out_shape=jax.ShapeDtypeStruct(spectra.shape, jnp.bfloat16),
+        out_shape=jax.ShapeDtypeStruct(spectra.shape, jnp.float32),
         compiler_params=pltpu.CompilerParams(vmem_limit_bytes=20 << 20),
         name="dequantize",
     )(spectra, lanes)
@@ -115,22 +115,24 @@
     return [(sr + ur, si + ui), (tr - vi, ti + vr), (sr - ur, si - ui), (tr + vi, ti - vr)]
 
 
-def lags_kernel(base, values_ref, slab_ref, twiddle_ref, high_ref, low_ref, out_ref, hi_ref, lo_ref, acc_ref):
+def lags_kernel(values_ref, slab_ref, twiddle_ref, high_ref, low_ref, out_ref, acc_ref, *parts):
     chans = out_ref.shape[1]
     segs = values_ref.shape[1]
     steps = SPAN // LANES
-
-    def produce(n, slot):
+    tall = RES * ROWS
+    slots = (parts[:4], parts[4:])
+
+    def produce(n, slot, begin=0, end=chans):
         def at(j):
             return pl.ds(pl.multiple_of(j * SPAN + n * LANES, LANES), LANES)
 
-        for r in range(0, chans, ROWS):
+        for r in range(begin, end, ROWS):
             x = []
             for j in range(RES // 2):
                 re = im = None
                 for g in range(segs):
-                    vr = values_ref[0, g, pl.ds(base + r, ROWS), at(j)].astype(jnp.float32)
-                    vi = values_ref[1, g, pl.ds(base + r, ROWS), at(j)].astype(jnp.float32)
+                    vr = values_ref[0, g, pl.ds(r, ROWS), at(j)]
+                    vi = values_ref[1, g, pl.ds(r, ROWS), at(j)]
                     sr = slab_ref[pl.ds(g, 1), at(j)]
                     si = slab_ref[pl.ds(segs + g, 1), at(j)]
                     pr = sr * vr + si * vi
@@ -154,68 +156,73 @@
                     cos = twiddle_ref[pl.ds(2 * u, 1), at(0)]
                     sin = twiddle_ref[pl.ds(2 * u + 1, 1), at(0)]
                     gr, gi = gr * cos - gi * sin, gr * sin + gi * cos
+                rows = pl.ds(r * RES + u * ROWS, ROWS)
                 for k, part in enumerate((gr, gi)):
                     top = part.astype(jnp.bfloat16)
-                    rest = (part - top.astype(jnp.float32)).astype(jnp.bfloat16)
-                    where = (slot, pl.ds(u * chans + r, ROWS), pl.ds(k * LANES, LANES))
-                    hi_ref[where] = top
-                    lo_ref[where] = rest
-
-    def contract(n, slot):
+                    slots[slot][k][rows, :] = top
+                    slots[slot][2 + k][rows, :] = (part - top.astype(jnp.float32)).astype(jnp.bfloat16)
+
+    def contract(n, slot, begin=0, end=chans):
+        piece = pl.ds(begin * RES, (end - begin) * RES)
         rows = pl.ds(pl.multiple_of(n * 2 * LANES, 2 * LANES), 2 * LANES)
-        whi = high_ref[rows, :]
-        hi = hi_ref[slot]
-        dot = lambda a, b: jnp.dot(a, b, preferred_element_type=jnp.float32)
-        return dot(hi, whi) + dot(lo_ref[slot], whi) + dot(hi, low_ref[rows, :])
-
+        table = jnp.concatenate([high_ref[rows, :], high_ref[rows, :], low_ref[rows, :]], axis=0)
+        hr, hi, lr, li = (ref[piece, :] for ref in slots[slot])
+        both = jnp.concatenate([hr, hi, lr, li, hr, hi], axis=1)
+        acc_ref[piece, :] += jnp.dot(both, table, preferred_element_type=jnp.float32)
+
+    acc_ref[...] = jnp.zeros_like(acc_ref)
     produce(0, 0)
-    acc_ref[...] = jnp.zeros_like(acc_ref)
 
     def step(n, carry):
-        produce(n, n % 2)
-        acc_ref[...] += contract(n - 1, (n - 1) % 2)
+        for slot in range(2):
+
+            @pl.when(n % 2 == slot)
+            def _():
+                for begin in range(0, chans, PIECE):
+                    contract(n - 1, 1 - slot, begin, begin + PIECE)
+                    produce(n, slot, begin, begin + PIECE)
+
         return carry
 
     lax.fori_loop(1, steps, step, 0)
-    acc_ref[...] += contract(steps - 1, (steps - 1) % 2)
-
     piece = COLS // RES
     per = LANES // piece
     lane = lax.broadcasted_iota(jnp.int32, (8, LANES), 1)
-    for r in range(0, chans, 8):
-        turned = []
-        for u in range(RES):
-            halves = [acc_ref[pl.ds(u * chans + r, 8), pl.ds(h * LANES, LANES)] for h in range(2)]
-            shift = piece * u
-            if shift >= LANES:
-                halves = halves[::-1]
-                shift -= LANES
-            if shift:
-                a, b = (pltpu.roll(x, shift, 1) for x in halves)
-                head = lane < shift
-                halves = [jnp.where(head, b, a), jnp.where(head, a, b)]
-            turned.append(halves)
-        for w in range(RES):
-            for h in range(2):
-                picks = [turned[(h * per + s - w) % RES][h] for s in range(per)]
-                left = jnp.where(lane < piece, picks[0], picks[1])
-                right = jnp.where(lane < 3 * piece, picks[2], picks[3])
-                out_ref[w, pl.ds(r, 8), pl.ds(h * LANES, LANES)] = jnp.where(lane < 2 * piece, left, right)
-
-
-def partial_lags(values, slab, tabs, base, chans):
+    for begin in range(0, chans, PIECE):
+        contract(steps - 1, (steps - 1) % 2, begin, begin + PIECE)
+        for r in range(begin, begin + PIECE, 8):
+            turned = []
+            for u in range(RES):
+                rows = pl.ds(r // ROWS * tall + u * ROWS + r % ROWS, 8)
+                halves = [acc_ref[rows, pl.ds(h * LANES, LANES)] for h in range(2)]
+                shift = piece * u
+                if shift >= LANES:
+                    halves = halves[::-1]
+                    shift -= LANES
+                if shift:
+                    a, b = (pltpu.roll(x, shift, 1) for x in halves)
+                    head = lane < shift
+                    halves = [jnp.where(head, b, a), jnp.where(head, a, b)]
+                turned.append(halves)
+            for w in range(RES):
+                for h in range(2):
+                    picks = [turned[(h * per + s - w) % RES][h] for s in range(per)]
+                    left = jnp.where(lane < piece, picks[0], picks[1])
+                    right = jnp.where(lane < 3 * piece, picks[2], picks[3])
+                    out_ref[w, pl.ds(r, 8), pl.ds(h * LANES, LANES)] = jnp.where(lane < 2 * piece, left, right)
+
+
+def partial_lags(values, slab, tabs):
+    chans = values.shape[2]
     high, low, twiddle = tabs
     vmem = pl.BlockSpec(memory_space=pltpu.VMEM)
     return pl.pallas_call(
-        lambda *refs: lags_kernel(base, *refs),
+        lags_kernel,
         in_specs=[vmem] * 5,
         out_specs=vmem,
         out_shape=jax.ShapeDtypeStruct((RES, chans, COLS), jnp.float32),
-        scratch_shapes=[
-            pltpu.VMEM((2, RES * chans, 2 * LANES), jnp.bfloat16),
-            pltpu.VMEM((2, RES * chans, 2 * LANES), jnp.bfloat16),
-            pltpu.VMEM((RES * chans, COLS), jnp.float32),
-        ],
+        scratch_shapes=[pltpu.VMEM((RES * chans, COLS), jnp.float32)]
+        + [pltpu.VMEM((RES * chans, LANES), jnp.bfloat16)] * 8,
         compiler_params=pltpu.CompilerParams(vmem_limit_bytes=16 << 20),
         name="lags",
     )(values, slab, twiddle, high, low)
@@ -251,7 +258,7 @@
 
 def spread(slab):
     peers = lax.axis_size("chan")
-    for bit in (1, 16, 2, 4, 8):
+    for bit in (1, 16, 2, 4, 12):
         slab = slab + lax.ppermute(slab, "chan", [(peer, peer ^ bit) for peer in range(peers)])
     return slab
 
@@ -266,7 +273,7 @@
     slab = spread(pick(local, spectra, lanes))
     values = dequantize(spectra, lanes)
     tabs = tables(1.0 / math.sqrt(4.0 * F * segs))
-    partial = partial_lags(values, slab, tabs, 0, chans)
+    partial = partial_lags(values, slab, tabs)
     tiles = lax.all_to_all(partial, "win", 0, 0, tiled=True)
     own = lax.axis_index("win").reshape(1).astype(jnp.int32)
     return finish(own, tiles)[None]

time: 56.9 us -> 55.8 us (0.981)
  starting transfers between devices: 20.5 us -> 19 us
    ppermute x5, starting transfers between devices: 15.4 us -> 13.9 us  [spread(): lax.ppermute(slab, 'chan', [(peer, peer ^ bit) for peer in range(peers)])]
  transfers between devices with their start and end apart: 6 -> 6, of which waited for: 5 -> 5; matrix products, arithmetic and copies ran while one was open for 0% -> 0% of each run, Pallas kernels for 5% -> 7%
where the time goes in v3:
time: 55.8 us; the launch traced here: 55.6 us
  waiting for transfers between devices  21.8 us (39%)
  starting transfers between devices  19 us (34%)
  Pallas kernels  13.9 us (25%)
  between operations  0.76 us (1%)
    ppermute x5, starting transfers between devices, spread(): lax.ppermute(slab, 'chan', [(peer, peer ^ bit) for peer in range(peers)])  13.9 us
    all_to_all x1, waiting for transfers between devices, body(): tiles = lax.all_to_all(partial, 'win', 0, 0, tiled=True)  12.4 us
    ppermute x5, waiting for transfers between devices, spread(): lax.ppermute(slab, 'chan', [(peer, peer ^ bit) for peer in range(peers)])  9.39 us
    pallas_call x1, Pallas kernels, partial_lags(): pl.pallas_call(lags_kernel, in_specs=[vmem] * 5, out_specs=vmem, out_shap...  7.33 us
    all_to_all x1, starting transfers between devices, body(): tiles = lax.all_to_all(partial, 'win', 0, 0, tiled=True)  5.12 us
    pallas_call x1, Pallas kernels, dequantize(): pl.pallas_call(dequantize_kernel, grid=(segs, 2), in_specs=[pl.BlockSpec(...  4.16 us
    pallas_call x1, Pallas kernels, pick(): pl.pallas_call(pick_kernel, in_specs=[pl.BlockSpec(memory_space=pltpu.SME...  1.47 us
  transfers between devices with their start and end apart: 6, of which 5 were waited for; matrix products, arithmetic and copies ran while one was open for 0% of the time, Pallas kernels for 7%

profile of v3, /device:TPU:4, one launch (start us, length us, event | category | flops | bytes accessed | tf_op | source)
XLA Modules:
  0.0 55.6 jit_solution(392065383973601543)
XLA Ops:
  0.7 0.0 copy-start
  0.7 0.0 copy-start.1
  0.7 0.0 copy-start.2
  0.7 1.5 %pick.1 = f32[4,4096]{1,0:T(4,128)S(1)} custom-call(s32[1]{0:T(128)S(6)} %sub.7.local_ref, bf16[2,2,128,4096]{3,2,1,0:T(8,128)(2,1)} %codes_ref.3, s32[2,32,128]{2,1,0:T(8,128)} %bitcast.4), custom_call_target="tpu_custom_call" | custom-call | tf_op jit(solution)/shard_map/pick/pallas_call | solution.py:91
  2.2 0.1 collective-permute-start
  2.3 1.2 %collective-permute-done = f32[4,4096]{1,0:T(4,128)S(1)} collective-permute-done((f32[4,4096]{1,0:T(4,128)S(1)}, f32[4,4096]{1,0:T(4,128)S(1)}, u32[]{:S(2)}, u32[]{:S(2)}) %collective-permute-start) | collective-permute-done | bytes 65568 | tf_op jit(solution)/shard_map/ppermute | solution.py:262
  3.5 2.3 %collective-permute-start.1 = (f32[4,4096]{1,0:T(4,128)S(1)}, f32[4,4096]{1,0:T(4,128)S(1)}, u32[]{:S(2)}, u32[]{:S(2)}) collective-permute-start(f32[4,4096]{1,0:T(4,128)S(1)} %add.15), channel_id=1, source_target_pairs={{0,128},{8,136},{16,144},{24,152},{32,160},{40,168},{48,176},{56,1... | collective-permute-start | bytes 196616 | tf_op jit(solution)/shard_map/ppermute | solution.py:262
  5.8 3.6 %collective-permute-done.1 = f32[4,4096]{1,0:T(4,128)S(1)} collective-permute-done((f32[4,4096]{1,0:T(4,128)S(1)}, f32[4,4096]{1,0:T(4,128)S(1)}, u32[]{:S(2)}, u32[]{:S(2)}) %collective-permute-start.1) | collective-permute-done | bytes 65568 | tf_op jit(solution)/shard_map/ppermute | solution.py:262
  9.4 2.0 %collective-permute-start.2 = (f32[4,4096]{1,0:T(4,128)S(1)}, f32[4,4096]{1,0:T(4,128)S(1)}, u32[]{:S(2)}, u32[]{:S(2)}) collective-permute-start(f32[4,4096]{1,0:T(4,128)S(1)} %add.16), channel_id=1, source_target_pairs={{0,16},{8,24},{16,0},{24,8},{32,48},{40,56},{48,32},{56,40},{64,80... | collective-permute-start | bytes 196616 | tf_op jit(solution)/shard_map/ppermute | solution.py:262
  11.4 2.3 %collective-permute-done.2 = f32[4,4096]{1,0:T(4,128)S(1)} collective-permute-done((f32[4,4096]{1,0:T(4,128)S(1)}, f32[4,4096]{1,0:T(4,128)S(1)}, u32[]{:S(2)}, u32[]{:S(2)}) %collective-permute-start.2) | collective-permute-done | bytes 65568 | tf_op jit(solution)/shard_map/ppermute | solution.py:262
  13.8 3.4 %collective-permute-start.3 = (f32[4,4096]{1,0:T(4,128)S(1)}, f32[4,4096]{1,0:T(4,128)S(1)}, u32[]{:S(2)}, u32[]{:S(2)}) collective-permute-start(f32[4,4096]{1,0:T(4,128)S(1)} %add.17), channel_id=1, source_target_pairs={{0,32},{8,40},{16,48},{24,56},{32,0},{40,8},{48,16},{56,24},{64,96... | collective-permute-start | bytes 196616 | tf_op jit(solution)/shard_map/ppermute | solution.py:262
  17.1 2.2 %collective-permute-done.3 = f32[4,4096]{1,0:T(4,128)S(1)} collective-permute-done((f32[4,4096]{1,0:T(4,128)S(1)}, f32[4,4096]{1,0:T(4,128)S(1)}, u32[]{:S(2)}, u32[]{:S(2)}) %collective-permute-start.3) | collective-permute-done | bytes 65568 | tf_op jit(solution)/shard_map/ppermute | solution.py:262
  19.4 6.1 %collective-permute-start.4 = (f32[4,4096]{1,0:T(4,128)S(1)}, f32[4,4096]{1,0:T(4,128)S(1)}, u32[]{:S(2)}, u32[]{:S(2)}) collective-permute-start(f32[4,4096]{1,0:T(4,128)S(1)} %add.18), channel_id=1, source_target_pairs={{0,96},{8,104},{16,112},{24,120},{32,64},{40,72},{48,80},{56,88},{... | collective-permute-start | bytes 196616 | tf_op jit(solution)/shard_map/ppermute | solution.py:262
  25.6 4.2 %dequantize.1.values_ref = f32[2,2,128,4096]{3,2,1,0:T(8,128)S(1)} custom-call(bf16[2,2,128,4096]{3,2,1,0:T(8,128)(2,1)} %codes_ref.3, s32[2,32,128]{2,1,0:T(8,128)} %bitcast.5), custom_call_target="tpu_custom_call" | custom-call | tf_op jit(solution)/shard_map/dequantize/pallas_call | solution.py:48
  29.7 0.0 collective-permute-done.4
  29.8 0.0 copy-done
  29.8 0.0 copy-done.1
  29.8 0.0 copy-done.2
  29.8 7.3 %lags.1 = f32[8,128,256]{2,1,0:T(8,128)} custom-call(f32[2,2,128,4096]{3,2,1,0:T(8,128)S(1)} %dequantize.1.values_ref, f32[4,4096]{1,0:T(4,128)S(1)} %add.19.slab_ref, f32[16,1024]{1,0:T(8,128)S(1)} %copy-done.2, bf16[2048,256]{1,0:T(8,128)(2,1)S(1)} %copy-done.1, bf16[2048,256]{1,0:T(8,128)(2,1)S(1)} %copy-done), custom_call_target="tpu_custom_call" | custom-call | tf_op jit(solution)/shard_map/lags/pallas_call | solution.py:219
  37.1 5.1 %all-to-all-start = ((f32[8,128,256]{2,1,0:T(8,128)}), f32[8,128,256]{2,1,0:T(8,128)S(1)}, u32[]{:S(2)}, u32[]{:S(2)}) async-start(f32[8,128,256]{2,1,0:T(8,128)} %lags.1), calls=%async_computation | async-start | bytes 2097152 | tf_op jit(solution)/shard_map/all_to_all | solution.py:277
  42.2 12.4 %all-to-all-done.tiles_ref = f32[8,128,256]{2,1,0:T(8,128)S(1)} async-done(((f32[8,128,256]{2,1,0:T(8,128)}), f32[8,128,256]{2,1,0:T(8,128)S(1)}, u32[]{:S(2)}, u32[]{:S(2)}) %all-to-all-start) | async-done | bytes 1048608 | tf_op jit(solution)/shard_map/all_to_all | solution.py:277
  54.6 0.9 %finish.1 = f32[128,256]{1,0:T(8,128)} custom-call(s32[1]{0:T(128)} %bitcast.own_ref, f32[8,128,256]{2,1,0:T(8,128)S(1)} %all-to-all-done.tiles_ref), custom_call_target="tpu_custom_call" | custom-call | tf_op jit(solution)/shard_map/finish/pallas_call | solution.py:249
  (5 shorter events, 0.1 us)
Async XLA Ops:
  0.7 29.1 %copy-start = (bf16[2048,256]{1,0:T(8,128)(2,1)S(1)}, bf16[2048,256]{1,0:T(8,128)(2,1)}, u32[]{:S(2)}) copy-start(bf16[2048,256]{1,0:T(8,128)(2,1)} %constant.19.clone.low_ref) | copy-start | bytes 3145732
  0.7 29.1 %copy-start.1 = (bf16[2048,256]{1,0:T(8,128)(2,1)S(1)}, bf16[2048,256]{1,0:T(8,128)(2,1)}, u32[]{:S(2)}) copy-start(bf16[2048,256]{1,0:T(8,128)(2,1)} %constant.18.clone.high_ref) | copy-start | bytes 3145732
  0.7 29.1 %copy-start.2 = (f32[16,1024]{1,0:T(8,128)S(1)}, f32[16,1024]{1,0:T(8,128)}, u32[]{:S(2)}) copy-start(f32[16,1024]{1,0:T(8,128)} %constant.17.clone.twiddle_ref) | copy-start | bytes 196612
  2.2 1.3 %collective-permute-start = (f32[4,4096]{1,0:T(4,128)S(1)}, f32[4,4096]{1,0:T(4,128)S(1)}, u32[]{:S(2)}, u32[]{:S(2)}) collective-permute-start(f32[4,4096]{1,0:T(4,128)S(1)} %pick.1), channel_id=1, source_target_pairs={{0,8},{8,0},{16,24},{24,16},{32,40},{40,32},{48,56},{56,48},{64,72... | collective-permute-start | bytes 196616 | tf_op jit(solution)/shard_map/ppermute | solution.py:262
  3.5 5.9 %collective-permute-start.1 = (f32[4,4096]{1,0:T(4,128)S(1)}, f32[4,4096]{1,0:T(4,128)S(1)}, u32[]{:S(2)}, u32[]{:S(2)}) collective-permute-start(f32[4,4096]{1,0:T(4,128)S(1)} %add.15), channel_id=1, source_target_pairs={{0,128},{8,136},{16,144},{24,152},{32,160},{40,168},{48,176},{56,1... | collective-permute-start | bytes 196616 | tf_op jit(solution)/shard_map/ppermute | solution.py:262
  9.4 4.4 %collective-permute-start.2 = (f32[4,4096]{1,0:T(4,128)S(1)}, f32[4,4096]{1,0:T(4,128)S(1)}, u32[]{:S(2)}, u32[]{:S(2)}) collective-permute-start(f32[4,4096]{1,0:T(4,128)S(1)} %add.16), channel_id=1, source_target_pairs={{0,16},{8,24},{16,0},{24,8},{32,48},{40,56},{48,32},{56,40},{64,80... | collective-permute-start | bytes 196616 | tf_op jit(solution)/shard_map/ppermute | solution.py:262
  13.8 5.6 %collective-permute-start.3 = (f32[4,4096]{1,0:T(4,128)S(1)}, f32[4,4096]{1,0:T(4,128)S(1)}, u32[]{:S(2)}, u32[]{:S(2)}) collective-permute-start(f32[4,4096]{1,0:T(4,128)S(1)} %add.17), channel_id=1, source_target_pairs={{0,32},{8,40},{16,48},{24,56},{32,0},{40,8},{48,16},{56,24},{64,96... | collective-permute-start | bytes 196616 | tf_op jit(solution)/shard_map/ppermute | solution.py:262
  19.4 10.3 %collective-permute-start.4 = (f32[4,4096]{1,0:T(4,128)S(1)}, f32[4,4096]{1,0:T(4,128)S(1)}, u32[]{:S(2)}, u32[]{:S(2)}) collective-permute-start(f32[4,4096]{1,0:T(4,128)S(1)} %add.18), channel_id=1, source_target_pairs={{0,96},{8,104},{16,112},{24,120},{32,64},{40,72},{48,80},{56,88},{... | collective-permute-start | bytes 196616 | tf_op jit(solution)/shard_map/ppermute | solution.py:262
  37.1 17.5 %all-to-all-start = ((f32[8,128,256]{2,1,0:T(8,128)}), f32[8,128,256]{2,1,0:T(8,128)S(1)}, u32[]{:S(2)}, u32[]{:S(2)}) async-start(f32[8,128,256]{2,1,0:T(8,128)} %lags.1), calls=%async_computation | async-start | bytes 2097152 | tf_op jit(solution)/shard_map/all_to_all | solution.py:277

commit v4 on v3

--- a/solution.py
+++ b/solution.py
@@ -34,23 +34,27 @@
 
 
 def dequantize_kernel(codes_ref, exponents_ref, values_ref):
-    seg, part = pl.program_id(0), pl.program_id(1)
+    seg, cut = pl.program_id(0), pl.program_id(1)
+    _, blocks, chans = exponents_ref.shape
     scale = jnp.exp2(exponents_ref[0].astype(jnp.float32)).T
-    for block in range(scale.shape[1]):
-        wide = jnp.broadcast_to(scale[:, block : block + 1], (scale.shape[0], LANES))
-        wide = wide.astype(jnp.bfloat16).astype(jnp.float32)
+    scale = scale.astype(jnp.bfloat16).astype(jnp.float32)
+    for block in range(blocks):
+        wide = jnp.broadcast_to(scale[:, block : block + 1], (chans, LANES))
         at = pl.ds(block * LANES, LANES)
-        values_ref[part, seg, :, at] = codes_ref[0, 0, :, at].astype(jnp.float32) * wide
+        to = pl.ds(pl.multiple_of((cut * blocks + block) * LANES, LANES), LANES)
+        for part in range(2):
+            values_ref[part, seg, :, to] = codes_ref[part, 0, :, at].astype(jnp.float32) * wide
 
 
 def dequantize(spectra, lanes):
     _, segs, chans, nbin = spectra.shape
+    cuts = 4
     return pl.pallas_call(
         dequantize_kernel,
-        grid=(segs, 2),
+        grid=(segs, cuts),
         in_specs=[
-            pl.BlockSpec((1, 1, chans, nbin), lambda g, p: (p, g, 0, 0)),
-            pl.BlockSpec((1, lanes.shape[1], chans), lambda g, p: (g, 0, 0)),
+            pl.BlockSpec((2, 1, chans, nbin // cuts), lambda g, k: (0, g, 0, k)),
+            pl.BlockSpec((1, lanes.shape[1] // cuts, chans), lambda g, k: (g, k, 0)),
         ],
         out_specs=pl.BlockSpec(memory_space=pltpu.VMEM),
         out_shape=jax.ShapeDtypeStruct(spectra.shape, jnp.float32),
@@ -59,9 +63,9 @@
     )(spectra, lanes)
 
 
-def pick_kernel(local_ref, codes_ref, exponents_ref, slab_ref, rows_ref, lanes_ref, row_sem, lane_sem):
+def pick_kernel(source_ref, codes_ref, exponents_ref, slab_ref, rows_ref, lanes_ref, row_sem, lane_sem):
     segs, blocks, chans = lanes_ref.shape
-    local = local_ref[0]
+    local = source_ref[0] - lax.axis_index("chan") * chans
     owned = (local >= 0) & (local < chans)
     row = jnp.clip(local, 0, chans - 1)
     first = pl.multiple_of(row // ROWS * ROWS, ROWS)
@@ -85,7 +89,7 @@
                 slab_ref[pl.ds(part * segs + g, 1), at] = code * scale[block : block + 1]
 
 
-def pick(local, spectra, lanes):
+def pick(source_channels, spectra, lanes):
     _, segs, _, nbin = spectra.shape
     hbm = pl.BlockSpec(memory_space=pltpu.MemorySpace.HBM)
     return pl.pallas_call(
@@ -101,7 +105,7 @@
         ],
         compiler_params=pltpu.CompilerParams(vmem_limit_bytes=4 << 20),
         name="pick",
-    )(local, spectra, lanes)
+    )(source_channels, spectra, lanes)
 
 
 def times_root(re, im):
@@ -228,14 +232,14 @@
     )(values, slab, twiddle, high, low)
 
 
-def finish_kernel(own_ref, tiles_ref, out_ref):
+def finish_kernel(tiles_ref, out_ref):
     total = tiles_ref[0]
     for peer in range(1, tiles_ref.shape[0]):
         total = total + tiles_ref[peer]
     piece = COLS // RES
     place = lax.broadcasted_iota(jnp.int32, (COLS, COLS), 0)
     lag = lax.broadcasted_iota(jnp.int32, (COLS, COLS), 1)
-    residue = (place // piece - own_ref[0] + RES) % RES
+    residue = (place // piece - lax.axis_index("win") + RES) % RES
     order = jnp.where(lag == place % piece * RES + residue, 1.0, 0.0).astype(jnp.bfloat16)
     first = total.astype(jnp.bfloat16)
     rest = total - first.astype(jnp.float32)
@@ -245,15 +249,15 @@
     out_ref[...] = (dot(third) + dot(second)) + dot(first)
 
 
-def finish(own, tiles):
+def finish(tiles):
     return pl.pallas_call(
         finish_kernel,
-        in_specs=[pl.BlockSpec(memory_space=pltpu.SMEM), pl.BlockSpec(memory_space=pltpu.VMEM)],
+        in_specs=[pl.BlockSpec(memory_space=pltpu.VMEM)],
         out_specs=pl.BlockSpec(memory_space=pltpu.VMEM),
         out_shape=jax.ShapeDtypeStruct(tiles.shape[1:], jnp.float32),
         compiler_params=pltpu.CompilerParams(vmem_limit_bytes=8 << 20),
         name="finish",
-    )(own, tiles)
+    )(tiles)
 
 
 def spread(slab):
@@ -264,19 +268,15 @@
 
 
 def body(spectra, exponents, source_channels):
-    chans = spectra.shape[2]
     segs = spectra.shape[1] * lax.axis_size("win")
     stay = lambda array: pltpu.with_memory_space_constraint(array, pltpu.MemorySpace.HBM)
     spectra = stay(spectra)
     lanes = stay(jnp.transpose(exponents, (0, 2, 1)))
-    local = source_channels - lax.axis_index("chan") * chans
-    slab = spread(pick(local, spectra, lanes))
+    slab = spread(pick(source_channels, spectra, lanes))
     values = dequantize(spectra, lanes)
     tabs = tables(1.0 / math.sqrt(4.0 * F * segs))
     partial = partial_lags(values, slab, tabs)
-    tiles = lax.all_to_all(partial, "win", 0, 0, tiled=True)
-    own = lax.axis_index("win").reshape(1).astype(jnp.int32)
-    return finish(own, tiles)[None]
+    return finish(lax.all_to_all(partial, "win", 0, 0, tiled=True))[None]
 
 
 def solution(mesh):

time: 55.8 us -> 56.6 us (1.014)
  blocking collectives: 0 us -> 17.2 us
  waiting for transfers between devices: 21.8 us -> 9.39 us
  starting transfers between devices: 19 us -> 13.9 us
  Pallas kernels: 13.9 us -> 15 us
    all_to_all x0 -> x1, blocking collectives: none -> 17.2 us  [body(): return finish(lax.all_to_all(partial, 'win', 0, 0, tiled=True))[None]]
    all_to_all x1 -> x0, waiting for transfers between devices: 12.4 us -> none  [body(): tiles = lax.all_to_all(partial, 'win', 0, 0, tiled=True)]
    all_to_all x1 -> x0, starting transfers between devices: 5.12 us -> none  [body(): tiles = lax.all_to_all(partial, 'win', 0, 0, tiled=True)]
    pallas_call x2, Pallas kernels: 5.11 us -> 7.16 us  [the longest x1 6.21 us: dequantize(): pl.pallas_call(dequantize_kernel, grid=(segs, cuts), in_specs=[pl.BlockSp...]
    pallas_call x1, Pallas kernels: 7.33 us -> 6.36 us  [partial_lags(): pl.pallas_call(lags_kernel, in_specs=[vmem] * 5, out_specs=vmem, out_shap...]
  transfers between devices with their start and end apart: 6 -> 5, of which waited for: 5 -> 4; matrix products, arithmetic and copies ran while one was open for 0% -> 0% of each run, Pallas kernels for 7% -> 11%
where the time goes in v4:
time: 56.6 us; the launch traced here: 56.3 us
  blocking collectives  17.2 us (30%)
  Pallas kernels  15 us (27%)
  starting transfers between devices  13.9 us (25%)
  waiting for transfers between devices  9.39 us (17%)
  between operations  0.76 us (1%)
    all_to_all x1, blocking collectives, body(): return finish(lax.all_to_all(partial, 'win', 0, 0, tiled=True))[None]  17.2 us
    ppermute x5, starting transfers between devices, spread(): lax.ppermute(slab, 'chan', [(peer, peer ^ bit) for peer in range(peers)])  13.9 us
    ppermute x5, waiting for transfers between devices, spread(): lax.ppermute(slab, 'chan', [(peer, peer ^ bit) for peer in range(peers)])  9.39 us
    pallas_call x1, Pallas kernels, partial_lags(): pl.pallas_call(lags_kernel, in_specs=[vmem] * 5, out_specs=vmem, out_shap...  6.36 us
    pallas_call x1, Pallas kernels, dequantize(): pl.pallas_call(dequantize_kernel, grid=(segs, cuts), in_specs=[pl.BlockSp...  6.21 us
    pallas_call x1, Pallas kernels, pick(): pl.pallas_call(pick_kernel, in_specs=[pl.BlockSpec(memory_space=pltpu.SME...  1.47 us
  transfers between devices with their start and end apart: 5, of which 4 were waited for; matrix products, arithmetic and copies ran while one was open for 0% of the time, Pallas kernels for 11%

profile of v4, /device:TPU:4, one launch (start us, length us, event | category | flops | bytes accessed | tf_op | source)
XLA Modules:
  0.0 56.3 jit_solution(497878792659000454)
XLA Ops:
  0.7 0.0 copy-start
  0.7 0.0 copy-start.1
  0.7 0.0 copy-start.2
  0.7 1.5 %pick.1 = f32[4,4096]{1,0:T(4,128)S(1)} custom-call(s32[1]{0:T(128)S(6)} %copy.7.source_ref, bf16[2,2,128,4096]{3,2,1,0:T(8,128)(2,1)} %codes_ref.3, s32[2,32,128]{2,1,0:T(8,128)} %bitcast.2), custom_call_target="tpu_custom_call" | custom-call | tf_op jit(solution)/shard_map/pick/pallas_call | solution.py:95
  2.2 0.1 collective-permute-start
  2.3 1.2 %collective-permute-done = f32[4,4096]{1,0:T(4,128)S(1)} collective-permute-done((f32[4,4096]{1,0:T(4,128)S(1)}, f32[4,4096]{1,0:T(4,128)S(1)}, u32[]{:S(2)}, u32[]{:S(2)}) %collective-permute-start) | collective-permute-done | bytes 65568 | tf_op jit(solution)/shard_map/ppermute | solution.py:266
  3.5 2.3 %collective-permute-start.1 = (f32[4,4096]{1,0:T(4,128)S(1)}, f32[4,4096]{1,0:T(4,128)S(1)}, u32[]{:S(2)}, u32[]{:S(2)}) collective-permute-start(f32[4,4096]{1,0:T(4,128)S(1)} %add.15), channel_id=1, source_target_pairs={{0,128},{8,136},{16,144},{24,152},{32,160},{40,168},{48,176},{56,1... | collective-permute-start | bytes 196616 | tf_op jit(solution)/shard_map/ppermute | solution.py:266
  5.8 3.6 %collective-permute-done.1 = f32[4,4096]{1,0:T(4,128)S(1)} collective-permute-done((f32[4,4096]{1,0:T(4,128)S(1)}, f32[4,4096]{1,0:T(4,128)S(1)}, u32[]{:S(2)}, u32[]{:S(2)}) %collective-permute-start.1) | collective-permute-done | bytes 65568 | tf_op jit(solution)/shard_map/ppermute | solution.py:266
  9.4 2.0 %collective-permute-start.2 = (f32[4,4096]{1,0:T(4,128)S(1)}, f32[4,4096]{1,0:T(4,128)S(1)}, u32[]{:S(2)}, u32[]{:S(2)}) collective-permute-start(f32[4,4096]{1,0:T(4,128)S(1)} %add.16), channel_id=1, source_target_pairs={{0,16},{8,24},{16,0},{24,8},{32,48},{40,56},{48,32},{56,40},{64,80... | collective-permute-start | bytes 196616 | tf_op jit(solution)/shard_map/ppermute | solution.py:266
  11.4 2.3 %collective-permute-done.2 = f32[4,4096]{1,0:T(4,128)S(1)} collective-permute-done((f32[4,4096]{1,0:T(4,128)S(1)}, f32[4,4096]{1,0:T(4,128)S(1)}, u32[]{:S(2)}, u32[]{:S(2)}) %collective-permute-start.2) | collective-permute-done | bytes 65568 | tf_op jit(solution)/shard_map/ppermute | solution.py:266
  13.8 3.4 %collective-permute-start.3 = (f32[4,4096]{1,0:T(4,128)S(1)}, f32[4,4096]{1,0:T(4,128)S(1)}, u32[]{:S(2)}, u32[]{:S(2)}) collective-permute-start(f32[4,4096]{1,0:T(4,128)S(1)} %add.17), channel_id=1, source_target_pairs={{0,32},{8,40},{16,48},{24,56},{32,0},{40,8},{48,16},{56,24},{64,96... | collective-permute-start | bytes 196616 | tf_op jit(solution)/shard_map/ppermute | solution.py:266
  17.1 2.2 %collective-permute-done.3 = f32[4,4096]{1,0:T(4,128)S(1)} collective-permute-done((f32[4,4096]{1,0:T(4,128)S(1)}, f32[4,4096]{1,0:T(4,128)S(1)}, u32[]{:S(2)}, u32[]{:S(2)}) %collective-permute-start.3) | collective-permute-done | bytes 65568 | tf_op jit(solution)/shard_map/ppermute | solution.py:266
  19.4 6.1 %collective-permute-start.4 = (f32[4,4096]{1,0:T(4,128)S(1)}, f32[4,4096]{1,0:T(4,128)S(1)}, u32[]{:S(2)}, u32[]{:S(2)}) collective-permute-start(f32[4,4096]{1,0:T(4,128)S(1)} %add.18), channel_id=1, source_target_pairs={{0,96},{8,104},{16,112},{24,120},{32,64},{40,72},{48,80},{56,88},{... | collective-permute-start | bytes 196616 | tf_op jit(solution)/shard_map/ppermute | solution.py:266
  25.6 6.2 %dequantize.1.values_ref = f32[2,2,128,4096]{3,2,1,0:T(8,128)S(1)} custom-call(bf16[2,2,128,4096]{3,2,1,0:T(8,128)(2,1)} %codes_ref.3, s32[2,32,128]{2,1,0:T(8,128)} %bitcast.3), custom_call_target="tpu_custom_call" | custom-call | tf_op jit(solution)/shard_map/dequantize/pallas_call | solution.py:52
  31.8 0.0 collective-permute-done.4
  31.8 0.0 copy-done
  31.8 0.0 copy-done.1
  31.8 0.0 copy-done.2
  31.8 6.4 %lags.1 = f32[8,128,256]{2,1,0:T(8,128)S(1)} custom-call(f32[2,2,128,4096]{3,2,1,0:T(8,128)S(1)} %dequantize.1.values_ref, f32[4,4096]{1,0:T(4,128)S(1)} %add.19.slab_ref, f32[16,1024]{1,0:T(8,128)S(1)} %copy-done.2, bf16[2048,256]{1,0:T(8,128)(2,1)S(1)} %copy-done.1, bf16[2048,256]{1,0:T(8,128)(2,1)S(1)} %copy-done), custom_call_target="tpu_custom_call" | custom-call | tf_op jit(solution)/shard_map/lags/pallas_call | solution.py:223
  38.2 17.2 %all_to_all.5.tiles_ref = f32[8,128,256]{2,1,0:T(8,128)S(1)} all-to-all(f32[8,128,256]{2,1,0:T(8,128)S(1)} %lags.1), channel_id=1, replica_groups=mesh['chan'=32,'win'=8] {'win'}, dimensions={0} | all-to-all | bytes 2097152 | tf_op jit(solution)/shard_map/all_to_all | solution.py:279
  55.4 1.0 %finish.1 = f32[128,256]{1,0:T(8,128)} custom-call(f32[8,128,256]{2,1,0:T(8,128)S(1)} %all_to_all.5.tiles_ref), custom_call_target="tpu_custom_call" | custom-call | tf_op jit(solution)/shard_map/finish/pallas_call | solution.py:253
  (5 shorter events, 0.1 us)
Async XLA Ops:
  0.7 31.2 %copy-start = (bf16[2048,256]{1,0:T(8,128)(2,1)S(1)}, bf16[2048,256]{1,0:T(8,128)(2,1)}, u32[]{:S(2)}) copy-start(bf16[2048,256]{1,0:T(8,128)(2,1)} %constant.8.clone.low_ref) | copy-start | bytes 3145732
  0.7 31.2 %copy-start.1 = (bf16[2048,256]{1,0:T(8,128)(2,1)S(1)}, bf16[2048,256]{1,0:T(8,128)(2,1)}, u32[]{:S(2)}) copy-start(bf16[2048,256]{1,0:T(8,128)(2,1)} %constant.7.clone.high_ref) | copy-start | bytes 3145732
  0.7 31.2 %copy-start.2 = (f32[16,1024]{1,0:T(8,128)S(1)}, f32[16,1024]{1,0:T(8,128)}, u32[]{:S(2)}) copy-start(f32[16,1024]{1,0:T(8,128)} %constant.6.clone.twiddle_ref) | copy-start | bytes 196612
  2.2 1.3 %collective-permute-start = (f32[4,4096]{1,0:T(4,128)S(1)}, f32[4,4096]{1,0:T(4,128)S(1)}, u32[]{:S(2)}, u32[]{:S(2)}) collective-permute-start(f32[4,4096]{1,0:T(4,128)S(1)} %pick.1), channel_id=1, source_target_pairs={{0,8},{8,0},{16,24},{24,16},{32,40},{40,32},{48,56},{56,48},{64,72... | collective-permute-start | bytes 196616 | tf_op jit(solution)/shard_map/ppermute | solution.py:266
  3.5 5.9 %collective-permute-start.1 = (f32[4,4096]{1,0:T(4,128)S(1)}, f32[4,4096]{1,0:T(4,128)S(1)}, u32[]{:S(2)}, u32[]{:S(2)}) collective-permute-start(f32[4,4096]{1,0:T(4,128)S(1)} %add.15), channel_id=1, source_target_pairs={{0,128},{8,136},{16,144},{24,152},{32,160},{40,168},{48,176},{56,1... | collective-permute-start | bytes 196616 | tf_op jit(solution)/shard_map/ppermute | solution.py:266
  9.4 4.4 %collective-permute-start.2 = (f32[4,4096]{1,0:T(4,128)S(1)}, f32[4,4096]{1,0:T(4,128)S(1)}, u32[]{:S(2)}, u32[]{:S(2)}) collective-permute-start(f32[4,4096]{1,0:T(4,128)S(1)} %add.16), channel_id=1, source_target_pairs={{0,16},{8,24},{16,0},{24,8},{32,48},{40,56},{48,32},{56,40},{64,80... | collective-permute-start | bytes 196616 | tf_op jit(solution)/shard_map/ppermute | solution.py:266
  13.8 5.6 %collective-permute-start.3 = (f32[4,4096]{1,0:T(4,128)S(1)}, f32[4,4096]{1,0:T(4,128)S(1)}, u32[]{:S(2)}, u32[]{:S(2)}) collective-permute-start(f32[4,4096]{1,0:T(4,128)S(1)} %add.17), channel_id=1, source_target_pairs={{0,32},{8,40},{16,48},{24,56},{32,0},{40,8},{48,16},{56,24},{64,96... | collective-permute-start | bytes 196616 | tf_op jit(solution)/shard_map/ppermute | solution.py:266
  19.4 12.4 %collective-permute-start.4 = (f32[4,4096]{1,0:T(4,128)S(1)}, f32[4,4096]{1,0:T(4,128)S(1)}, u32[]{:S(2)}, u32[]{:S(2)}) collective-permute-start(f32[4,4096]{1,0:T(4,128)S(1)} %add.18), channel_id=1, source_target_pairs={{0,96},{8,104},{16,112},{24,120},{32,64},{40,72},{48,80},{56,88},{... | collective-permute-start | bytes 196616 | tf_op jit(solution)/shard_map/ppermute | solution.py:266

commit v5 on v4

--- a/solution.py
+++ b/solution.py
@@ -34,31 +34,28 @@
 
 
 def dequantize_kernel(codes_ref, exponents_ref, values_ref):
-    seg, cut = pl.program_id(0), pl.program_id(1)
+    part = pl.program_id(0)
     _, blocks, chans = exponents_ref.shape
     scale = jnp.exp2(exponents_ref[0].astype(jnp.float32)).T
     scale = scale.astype(jnp.bfloat16).astype(jnp.float32)
     for block in range(blocks):
         wide = jnp.broadcast_to(scale[:, block : block + 1], (chans, LANES))
         at = pl.ds(block * LANES, LANES)
-        to = pl.ds(pl.multiple_of((cut * blocks + block) * LANES, LANES), LANES)
-        for part in range(2):
-            values_ref[part, seg, :, to] = codes_ref[part, 0, :, at].astype(jnp.float32) * wide
-
-
-def dequantize(spectra, lanes):
-    _, segs, chans, nbin = spectra.shape
-    cuts = 4
+        values_ref[part, :, at] = codes_ref[0, 0, :, at].astype(jnp.float32) * wide
+
+
+def dequantize(spectra, lanes, seg):
+    _, _, chans, nbin = spectra.shape
     return pl.pallas_call(
         dequantize_kernel,
-        grid=(segs, cuts),
+        grid=(2,),
         in_specs=[
-            pl.BlockSpec((2, 1, chans, nbin // cuts), lambda g, k: (0, g, 0, k)),
-            pl.BlockSpec((1, lanes.shape[1] // cuts, chans), lambda g, k: (g, k, 0)),
+            pl.BlockSpec((1, 1, chans, nbin), lambda p: (p, seg, 0, 0)),
+            pl.BlockSpec((1, *lanes.shape[1:]), lambda p: (seg, 0, 0)),
         ],
         out_specs=pl.BlockSpec(memory_space=pltpu.VMEM),
-        out_shape=jax.ShapeDtypeStruct(spectra.shape, jnp.float32),
-        compiler_params=pltpu.CompilerParams(vmem_limit_bytes=20 << 20),
+        out_shape=jax.ShapeDtypeStruct((2, chans, nbin), jnp.float32),
+        compiler_params=pltpu.CompilerParams(vmem_limit_bytes=8 << 20),
         name="dequantize",
     )(spectra, lanes)
 
@@ -119,9 +116,10 @@
     return [(sr + ur, si + ui), (tr - vi, ti + vr), (sr - ur, si - ui), (tr + vi, ti - vr)]
 
 
-def lags_kernel(values_ref, slab_ref, twiddle_ref, high_ref, low_ref, out_ref, acc_ref, *parts):
+def lags_kernel(first_ref, second_ref, slab_ref, twiddle_ref, high_ref, low_ref, out_ref, acc_ref, *parts):
     chans = out_ref.shape[1]
-    segs = values_ref.shape[1]
+    values = (first_ref, second_ref)
+    segs = len(values)
     steps = SPAN // LANES
     tall = RES * ROWS
     slots = (parts[:4], parts[4:])
@@ -135,8 +133,8 @@
             for j in range(RES // 2):
                 re = im = None
                 for g in range(segs):
-                    vr = values_ref[0, g, pl.ds(r, ROWS), at(j)]
-                    vi = values_ref[1, g, pl.ds(r, ROWS), at(j)]
+                    vr = values[g][0, pl.ds(r, ROWS), at(j)]
+                    vi = values[g][1, pl.ds(r, ROWS), at(j)]
                     sr = slab_ref[pl.ds(g, 1), at(j)]
                     si = slab_ref[pl.ds(segs + g, 1), at(j)]
                     pr = sr * vr + si * vi
@@ -217,19 +215,19 @@
 
 
 def partial_lags(values, slab, tabs):
-    chans = values.shape[2]
+    chans = values[0].shape[1]
     high, low, twiddle = tabs
     vmem = pl.BlockSpec(memory_space=pltpu.VMEM)
     return pl.pallas_call(
         lags_kernel,
-        in_specs=[vmem] * 5,
+        in_specs=[vmem] * 6,
         out_specs=vmem,
         out_shape=jax.ShapeDtypeStruct((RES, chans, COLS), jnp.float32),
         scratch_shapes=[pltpu.VMEM((RES * chans, COLS), jnp.float32)]
         + [pltpu.VMEM((RES * chans, LANES), jnp.bfloat16)] * 8,
         compiler_params=pltpu.CompilerParams(vmem_limit_bytes=16 << 20),
         name="lags",
-    )(values, slab, twiddle, high, low)
+    )(*values, slab, twiddle, high, low)
 
 
 def finish_kernel(tiles_ref, out_ref):
@@ -260,11 +258,9 @@
     )(tiles)
 
 
-def spread(slab):
+def exchange(slab, bit):
     peers = lax.axis_size("chan")
-    for bit in (1, 16, 2, 4, 12):
-        slab = slab + lax.ppermute(slab, "chan", [(peer, peer ^ bit) for peer in range(peers)])
-    return slab
+    return slab + lax.ppermute(slab, "chan", [(peer, peer ^ bit) for peer in range(peers)])
 
 
 def body(spectra, exponents, source_channels):
@@ -272,10 +268,13 @@
     stay = lambda array: pltpu.with_memory_space_constraint(array, pltpu.MemorySpace.HBM)
     spectra = stay(spectra)
     lanes = stay(jnp.transpose(exponents, (0, 2, 1)))
-    slab = spread(pick(source_channels, spectra, lanes))
-    values = dequantize(spectra, lanes)
+    slab = exchange(pick(source_channels, spectra, lanes), 1)
+    slab, first = lax.optimization_barrier((exchange(slab, 16), dequantize(spectra, lanes, 0)))
+    slab = exchange(slab, 2)
+    slab, second = lax.optimization_barrier((exchange(slab, 4), dequantize(spectra, lanes, 1)))
+    slab = exchange(slab, 12)
     tabs = tables(1.0 / math.sqrt(4.0 * F * segs))
-    partial = partial_lags(values, slab, tabs)
+    partial = partial_lags((first, second), slab, tabs)
     return finish(lax.all_to_all(partial, "win", 0, 0, tiled=True))[None]
 
 

time: 56.6 us -> 52.4 us (0.926)
  waiting for transfers between devices: 9.39 us -> 7.17 us
  Pallas kernels: 15 us -> 13.2 us
    ppermute x5, waiting for transfers between devices: 9.39 us -> 7.17 us  [exchange(): lax.ppermute(slab, 'chan', [(peer, peer ^ bit) for peer in range(peers)])]
    pallas_call x2 -> x3, Pallas kernels: 12.6 us -> 10.9 us  [the longest x1 6.36 us: partial_lags(): pl.pallas_call(lags_kernel, in_specs=[vmem] * 6, out_specs=vmem, out_shap...]
  transfers between devices with their start and end apart: 5 -> 5, of which waited for: 4 -> 4; matrix products, arithmetic and copies ran while one was open for 0% -> 0% of each run, Pallas kernels for 11% -> 9%
where the time goes in v5:
time: 52.4 us; the launch traced here: 52.2 us
  blocking collectives  17.1 us (33%)
  starting transfers between devices  13.8 us (26%)
  Pallas kernels  13.2 us (25%)
  waiting for transfers between devices  7.17 us (14%)
  between operations  0.77 us (1%)
    all_to_all x1, blocking collectives, body(): return finish(lax.all_to_all(partial, 'win', 0, 0, tiled=True))[None]  17.1 us
    ppermute x5, starting transfers between devices, exchange(): lax.ppermute(slab, 'chan', [(peer, peer ^ bit) for peer in range(peers)])  13.8 us
    ppermute x5, waiting for transfers between devices, exchange(): lax.ppermute(slab, 'chan', [(peer, peer ^ bit) for peer in range(peers)])  7.17 us
    pallas_call x1, Pallas kernels, partial_lags(): pl.pallas_call(lags_kernel, in_specs=[vmem] * 6, out_specs=vmem, out_shap...  6.36 us
    pallas_call x2, Pallas kernels, dequantize(): pl.pallas_call(dequantize_kernel, grid=(2,), in_specs=[pl.BlockSpec((1, 1...  4.55 us
    pallas_call x1, Pallas kernels, pick(): pl.pallas_call(pick_kernel, in_specs=[pl.BlockSpec(memory_space=pltpu.SME...  1.33 us
  transfers between devices with their start and end apart: 5, of which 4 were waited for; matrix products, arithmetic and copies ran while one was open for 0% of the time, Pallas kernels for 9%

profile of v5, /device:TPU:4, one launch (start us, length us, event | category | flops | bytes accessed | tf_op | source)
XLA Modules:
  0.0 52.2 jit_solution(13386543388247349435)
XLA Ops:
  0.7 1.3 %pick.1 = f32[4,4096]{1,0:T(4,128)S(1)} custom-call(s32[1]{0:T(128)S(6)} %copy.7.source_ref, bf16[2,2,128,4096]{3,2,1,0:T(8,128)(2,1)} %codes_ref.5, s32[2,32,128]{2,1,0:T(8,128)} %bitcast.2), custom_call_target="tpu_custom_call" | custom-call | tf_op jit(solution)/shard_map/pick/pallas_call | solution.py:92
  2.0 0.1 collective-permute-start
  2.1 1.2 %collective-permute-done = f32[4,4096]{1,0:T(4,128)S(1)} collective-permute-done((f32[4,4096]{1,0:T(4,128)S(1)}, f32[4,4096]{1,0:T(4,128)S(1)}, u32[]{:S(2)}, u32[]{:S(2)}) %collective-permute-start) | collective-permute-done | bytes 65568 | tf_op jit(solution)/shard_map/ppermute | solution.py:263
  3.4 2.3 %collective-permute-start.1 = (f32[4,4096]{1,0:T(4,128)S(1)}, f32[4,4096]{1,0:T(4,128)S(1)}, u32[]{:S(2)}, u32[]{:S(2)}) collective-permute-start(f32[4,4096]{1,0:T(4,128)S(1)} %add.15), channel_id=1, source_target_pairs={{0,128},{8,136},{16,144},{24,152},{32,160},{40,168},{48,176},{56,1... | collective-permute-start | bytes 196616 | tf_op jit(solution)/shard_map/ppermute | solution.py:263
  5.7 2.3 %dequantize.2.first_ref = f32[2,128,4096]{2,1,0:T(8,128)S(1)} custom-call(bf16[2,2,128,4096]{3,2,1,0:T(8,128)(2,1)} %codes_ref.5, s32[2,32,128]{2,1,0:T(8,128)} %bitcast.3), custom_call_target="tpu_custom_call" | custom-call | tf_op jit(solution)/shard_map/dequantize/pallas_call | solution.py:49
  7.9 1.3 %collective-permute-done.1 = f32[4,4096]{1,0:T(4,128)S(1)} collective-permute-done((f32[4,4096]{1,0:T(4,128)S(1)}, f32[4,4096]{1,0:T(4,128)S(1)}, u32[]{:S(2)}, u32[]{:S(2)}) %collective-permute-start.1) | collective-permute-done | bytes 65568 | tf_op jit(solution)/shard_map/ppermute | solution.py:263
  9.2 2.0 %collective-permute-start.2 = (f32[4,4096]{1,0:T(4,128)S(1)}, f32[4,4096]{1,0:T(4,128)S(1)}, u32[]{:S(2)}, u32[]{:S(2)}) collective-permute-start(f32[4,4096]{1,0:T(4,128)S(1)} %add.16), channel_id=1, source_target_pairs={{0,16},{8,24},{16,0},{24,8},{32,48},{40,56},{48,32},{56,40},{64,80... | collective-permute-start | bytes 196616 | tf_op jit(solution)/shard_map/ppermute | solution.py:263
  11.2 2.3 %collective-permute-done.2 = f32[4,4096]{1,0:T(4,128)S(1)} collective-permute-done((f32[4,4096]{1,0:T(4,128)S(1)}, f32[4,4096]{1,0:T(4,128)S(1)}, u32[]{:S(2)}, u32[]{:S(2)}) %collective-permute-start.2) | collective-permute-done | bytes 65568 | tf_op jit(solution)/shard_map/ppermute | solution.py:263
  13.6 0.0 copy-start
  13.6 0.0 copy-start.1
  13.6 0.0 copy-start.2
  13.6 3.4 %collective-permute-start.3 = (f32[4,4096]{1,0:T(4,128)S(1)}, f32[4,4096]{1,0:T(4,128)S(1)}, u32[]{:S(2)}, u32[]{:S(2)}) collective-permute-start(f32[4,4096]{1,0:T(4,128)S(1)} %add.17), channel_id=1, source_target_pairs={{0,32},{8,40},{16,48},{24,56},{32,0},{40,8},{48,16},{56,24},{64,96... | collective-permute-start | bytes 196616 | tf_op jit(solution)/shard_map/ppermute | solution.py:263
  17.0 2.3 %dequantize.3.second_ref = f32[2,128,4096]{2,1,0:T(8,128)S(1)} custom-call(bf16[2,2,128,4096]{3,2,1,0:T(8,128)(2,1)} %codes_ref.5, s32[2,32,128]{2,1,0:T(8,128)} %bitcast.4), custom_call_target="tpu_custom_call" | custom-call | tf_op jit(solution)/shard_map/dequantize/pallas_call | solution.py:49
  19.3 0.0 collective-permute-done.3
  19.3 6.1 %collective-permute-start.4 = (f32[4,4096]{1,0:T(4,128)S(1)}, f32[4,4096]{1,0:T(4,128)S(1)}, u32[]{:S(2)}, u32[]{:S(2)}) collective-permute-start(f32[4,4096]{1,0:T(4,128)S(1)} %add.18), channel_id=1, source_target_pairs={{0,96},{8,104},{16,112},{24,120},{32,64},{40,72},{48,80},{56,88},{... | collective-permute-start | bytes 196616 | tf_op jit(solution)/shard_map/ppermute | solution.py:263
  25.4 2.3 %collective-permute-done.4 = f32[4,4096]{1,0:T(4,128)S(1)} collective-permute-done((f32[4,4096]{1,0:T(4,128)S(1)}, f32[4,4096]{1,0:T(4,128)S(1)}, u32[]{:S(2)}, u32[]{:S(2)}) %collective-permute-start.4) | collective-permute-done | bytes 65568 | tf_op jit(solution)/shard_map/ppermute | solution.py:263
  27.7 0.0 copy-done
  27.7 0.0 copy-done.1
  27.7 0.0 copy-done.2
  27.8 6.4 %lags.1 = f32[8,128,256]{2,1,0:T(8,128)S(1)} custom-call(f32[2,128,4096]{2,1,0:T(8,128)S(1)} %dequantize.2.first_ref, f32[2,128,4096]{2,1,0:T(8,128)S(1)} %dequantize.3.second_ref, f32[4,4096]{1,0:T(4,128)S(1)} %add.19.slab_ref, f32[16,1024]{1,0:T(8,128)S(1)} %copy-done.2, bf16[2048,256]{1,0:T(8,128)(2,1)S(1)} %copy-done.1, bf16[2048,256]{1,0:T(8,128)(2,1)S(1)} %copy-done), custom_call_target="tpu_custom_call" | custom-call | tf_op jit(solution)/shard_map/lags/pallas_call | solution.py:221
  34.1 17.1 %all_to_all.5.tiles_ref = f32[8,128,256]{2,1,0:T(8,128)S(1)} all-to-all(f32[8,128,256]{2,1,0:T(8,128)S(1)} %lags.1), channel_id=1, replica_groups=mesh['chan'=32,'win'=8] {'win'}, dimensions={0} | all-to-all | bytes 2097152 | tf_op jit(solution)/shard_map/all_to_all | solution.py:278
  51.2 1.0 %finish.1 = f32[128,256]{1,0:T(8,128)} custom-call(f32[8,128,256]{2,1,0:T(8,128)S(1)} %all_to_all.5.tiles_ref), custom_call_target="tpu_custom_call" | custom-call | tf_op jit(solution)/shard_map/finish/pallas_call | solution.py:251
  (5 shorter events, 0.1 us)
Async XLA Ops:
  2.0 1.3 %collective-permute-start = (f32[4,4096]{1,0:T(4,128)S(1)}, f32[4,4096]{1,0:T(4,128)S(1)}, u32[]{:S(2)}, u32[]{:S(2)}) collective-permute-start(f32[4,4096]{1,0:T(4,128)S(1)} %pick.1), channel_id=1, source_target_pairs={{0,8},{8,0},{16,24},{24,16},{32,40},{40,32},{48,56},{56,48},{64,72... | collective-permute-start | bytes 196616 | tf_op jit(solution)/shard_map/ppermute | solution.py:263
  3.4 5.9 %collective-permute-start.1 = (f32[4,4096]{1,0:T(4,128)S(1)}, f32[4,4096]{1,0:T(4,128)S(1)}, u32[]{:S(2)}, u32[]{:S(2)}) collective-permute-start(f32[4,4096]{1,0:T(4,128)S(1)} %add.15), channel_id=1, source_target_pairs={{0,128},{8,136},{16,144},{24,152},{32,160},{40,168},{48,176},{56,1... | collective-permute-start | bytes 196616 | tf_op jit(solution)/shard_map/ppermute | solution.py:263
  9.2 4.4 %collective-permute-start.2 = (f32[4,4096]{1,0:T(4,128)S(1)}, f32[4,4096]{1,0:T(4,128)S(1)}, u32[]{:S(2)}, u32[]{:S(2)}) collective-permute-start(f32[4,4096]{1,0:T(4,128)S(1)} %add.16), channel_id=1, source_target_pairs={{0,16},{8,24},{16,0},{24,8},{32,48},{40,56},{48,32},{56,40},{64,80... | collective-permute-start | bytes 196616 | tf_op jit(solution)/shard_map/ppermute | solution.py:263
  13.6 14.1 %copy-start = (bf16[2048,256]{1,0:T(8,128)(2,1)S(1)}, bf16[2048,256]{1,0:T(8,128)(2,1)}, u32[]{:S(2)}) copy-start(bf16[2048,256]{1,0:T(8,128)(2,1)} %constant.8.clone.low_ref) | copy-start | bytes 3145732
  13.6 14.1 %copy-start.1 = (bf16[2048,256]{1,0:T(8,128)(2,1)S(1)}, bf16[2048,256]{1,0:T(8,128)(2,1)}, u32[]{:S(2)}) copy-start(bf16[2048,256]{1,0:T(8,128)(2,1)} %constant.7.clone.high_ref) | copy-start | bytes 3145732
  13.6 14.1 %copy-start.2 = (f32[16,1024]{1,0:T(8,128)S(1)}, f32[16,1024]{1,0:T(8,128)}, u32[]{:S(2)}) copy-start(f32[16,1024]{1,0:T(8,128)} %constant.6.clone.twiddle_ref) | copy-start | bytes 196612
  13.6 5.6 %collective-permute-start.3 = (f32[4,4096]{1,0:T(4,128)S(1)}, f32[4,4096]{1,0:T(4,128)S(1)}, u32[]{:S(2)}, u32[]{:S(2)}) collective-permute-start(f32[4,4096]{1,0:T(4,128)S(1)} %add.17), channel_id=1, source_target_pairs={{0,32},{8,40},{16,48},{24,56},{32,0},{40,8},{48,16},{56,24},{64,96... | collective-permute-start | bytes 196616 | tf_op jit(solution)/shard_map/ppermute | solution.py:263
  19.3 8.4 %collective-permute-start.4 = (f32[4,4096]{1,0:T(4,128)S(1)}, f32[4,4096]{1,0:T(4,128)S(1)}, u32[]{:S(2)}, u32[]{:S(2)}) collective-permute-start(f32[4,4096]{1,0:T(4,128)S(1)} %add.18), channel_id=1, source_target_pairs={{0,96},{8,104},{16,112},{24,120},{32,64},{40,72},{48,80},{56,88},{... | collective-permute-start | bytes 196616 | tf_op jit(solution)/shard_map/ppermute | solution.py:263

commit v6 on v5

--- a/solution.py
+++ b/solution.py
@@ -1,3 +1,4 @@
+import functools
 import math
 
 import jax
@@ -16,6 +17,8 @@
 LANES = 128
 ROWS = 16
 PIECE = 32
+EIGHT = 8
+CORES = 2
 ROOT = math.sqrt(0.5)
 
 
@@ -60,43 +63,56 @@
     )(spectra, lanes)
 
 
-def pick_kernel(source_ref, codes_ref, exponents_ref, slab_ref, rows_ref, lanes_ref, row_sem, lane_sem):
+def core_of():
+    return lax.axis_index("chan") % CORES
+
+
+def pick_kernel(source_ref, codes_ref, exponents_ref, keep_ref, give_ref, rows_ref, lanes_ref, slab_ref, row_sem, lane_sem):
     segs, blocks, chans = lanes_ref.shape
     local = source_ref[0] - lax.axis_index("chan") * chans
     owned = (local >= 0) & (local < chans)
     row = jnp.clip(local, 0, chans - 1)
-    first = pl.multiple_of(row // ROWS * ROWS, ROWS)
-    rows_in = pltpu.make_async_copy(codes_ref.at[:, :, pl.ds(first, ROWS), :], rows_ref, row_sem)
+    first = pl.multiple_of(row // EIGHT * EIGHT, EIGHT)
+    rows_in = pltpu.make_async_copy(codes_ref.at[:, :, pl.ds(first, EIGHT), :], rows_ref, row_sem)
     lanes_in = pltpu.make_async_copy(exponents_ref, lanes_ref, lane_sem)
     rows_in.start()
     lanes_in.start()
     own_lane = lax.broadcasted_iota(jnp.int32, (blocks, chans), 1) == row
-    own_row = lax.broadcasted_iota(jnp.int32, (ROWS, LANES), 0) == row % ROWS
+    own_row = lax.broadcasted_iota(jnp.int32, (EIGHT, LANES), 0) == row % EIGHT
     lanes_in.wait()
     rows_in.wait()
+    groups = SPAN // LANES
+    part_groups = groups // CORES
     for g in range(segs):
         exponent = jnp.sum(jnp.where(own_lane, lanes_ref[g].astype(jnp.float32), 0.0), axis=1, keepdims=True)
         scale = jnp.where(owned, jnp.exp2(exponent), 0.0)
         scale = jnp.broadcast_to(scale, (blocks, LANES)).astype(jnp.bfloat16).astype(jnp.float32)
         for part in range(2):
             for block in range(blocks):
-                at = pl.ds(block * LANES, LANES)
-                codes = rows_ref[part, g, :, at].astype(jnp.float32)
+                codes = rows_ref[part, g, :, pl.ds(block * LANES, LANES)].astype(jnp.float32)
                 code = jnp.sum(jnp.where(own_row, codes, 0.0), axis=0, keepdims=True)
-                slab_ref[pl.ds(part * segs + g, 1), at] = code * scale[block : block + 1]
+                j, group = divmod(block, groups)
+                half, inner = divmod(group, part_groups)
+                to = pl.ds((j * part_groups + inner) * LANES, LANES)
+                slab_ref[half, pl.ds(part * segs + g, 1), to] = code * scale[block : block + 1]
+    keep_ref[...] = slab_ref[core_of()]
+    give_ref[...] = slab_ref[CORES - 1 - core_of()]
 
 
 def pick(source_channels, spectra, lanes):
     _, segs, _, nbin = spectra.shape
     hbm = pl.BlockSpec(memory_space=pltpu.MemorySpace.HBM)
+    vmem = pl.BlockSpec(memory_space=pltpu.VMEM)
+    half = jax.ShapeDtypeStruct((2 * segs, nbin // CORES), jnp.float32)
     return pl.pallas_call(
         pick_kernel,
         in_specs=[pl.BlockSpec(memory_space=pltpu.SMEM), hbm, hbm],
-        out_specs=pl.BlockSpec(memory_space=pltpu.VMEM),
-        out_shape=jax.ShapeDtypeStruct((2 * segs, nbin), jnp.float32),
+        out_specs=(vmem, vmem),
+        out_shape=(half, half),
         scratch_shapes=[
-            pltpu.VMEM((2, segs, ROWS, nbin), jnp.bfloat16),
+            pltpu.VMEM((2, segs, EIGHT, nbin), jnp.bfloat16),
             pltpu.VMEM(lanes.shape, jnp.int32),
+            pltpu.VMEM((CORES, *half.shape), jnp.float32),
             pltpu.SemaphoreType.DMA(()),
             pltpu.SemaphoreType.DMA(()),
         ],
@@ -116,17 +132,26 @@
     return [(sr + ur, si + ui), (tr - vi, ti + vr), (sr - ur, si - ui), (tr + vi, ti - vr)]
 
 
-def lags_kernel(first_ref, second_ref, slab_ref, twiddle_ref, high_ref, low_ref, out_ref, acc_ref, *parts):
-    chans = out_ref.shape[1]
+def lags_kernel(last, first_ref, second_ref, slab_ref, twiddle_ref, high_ref, low_ref, *refs):
+    if last:
+        sum_ref, out_ref, acc_ref, *parts = refs
+        half = CORES - 1 - core_of()
+    else:
+        acc_ref, *parts = refs
+        half = core_of()
     values = (first_ref, second_ref)
     segs = len(values)
-    steps = SPAN // LANES
+    chans = first_ref.shape[1]
+    steps = SPAN // LANES // CORES
     tall = RES * ROWS
     slots = (parts[:4], parts[4:])
 
     def produce(n, slot, begin=0, end=chans):
         def at(j):
-            return pl.ds(pl.multiple_of(j * SPAN + n * LANES, LANES), LANES)
+            return pl.ds(pl.multiple_of(j * SPAN + (half * steps + n) * LANES, LANES), LANES)
+
+        def slab_at(j):
+            return pl.ds(pl.multiple_of((j * steps + n) * LANES, LANES), LANES)
 
         for r in range(begin, end, ROWS):
             x = []
@@ -135,8 +160,8 @@
                 for g in range(segs):
                     vr = values[g][0, pl.ds(r, ROWS), at(j)]
                     vi = values[g][1, pl.ds(r, ROWS), at(j)]
-                    sr = slab_ref[pl.ds(g, 1), at(j)]
-                    si = slab_ref[pl.ds(segs + g, 1), at(j)]
+                    sr = slab_ref[pl.ds(g, 1), slab_at(j)]
+                    si = slab_ref[pl.ds(segs + g, 1), slab_at(j)]
                     pr = sr * vr + si * vi
                     pi = sr * vi - si * vr
                     re = pr if re is None else re + pr
@@ -166,13 +191,13 @@
 
     def contract(n, slot, begin=0, end=chans):
         piece = pl.ds(begin * RES, (end - begin) * RES)
-        rows = pl.ds(pl.multiple_of(n * 2 * LANES, 2 * LANES), 2 * LANES)
+        rows = pl.ds(pl.multiple_of((half * steps + n) * 2 * LANES, 2 * LANES), 2 * LANES)
         table = jnp.concatenate([high_ref[rows, :], high_ref[rows, :], low_ref[rows, :]], axis=0)
         hr, hi, lr, li = (ref[piece, :] for ref in slots[slot])
         both = jnp.concatenate([hr, hi, lr, li, hr, hi], axis=1)
         acc_ref[piece, :] += jnp.dot(both, table, preferred_element_type=jnp.float32)
 
-    acc_ref[...] = jnp.zeros_like(acc_ref)
+    acc_ref[...] = sum_ref[...] if last else jnp.zeros_like(acc_ref)
     produce(0, 0)
 
     def step(n, carry):
@@ -192,6 +217,8 @@
     lane = lax.broadcasted_iota(jnp.int32, (8, LANES), 1)
     for begin in range(0, chans, PIECE):
         contract(steps - 1, (steps - 1) % 2, begin, begin + PIECE)
+        if not last:
+            continue
         for r in range(begin, begin + PIECE, 8):
             turned = []
             for u in range(RES):
@@ -214,20 +241,22 @@
                     out_ref[w, pl.ds(r, 8), pl.ds(h * LANES, LANES)] = jnp.where(lane < 2 * piece, left, right)
 
 
-def partial_lags(values, slab, tabs):
+def partial_lags(values, slab, tabs, total=None):
     chans = values[0].shape[1]
     high, low, twiddle = tabs
     vmem = pl.BlockSpec(memory_space=pltpu.VMEM)
+    last = total is not None
+    sums = (RES * chans, COLS)
     return pl.pallas_call(
-        lags_kernel,
-        in_specs=[vmem] * 6,
+        functools.partial(lags_kernel, last),
+        in_specs=[vmem] * (7 if last else 6),
         out_specs=vmem,
-        out_shape=jax.ShapeDtypeStruct((RES, chans, COLS), jnp.float32),
-        scratch_shapes=[pltpu.VMEM((RES * chans, COLS), jnp.float32)]
+        out_shape=jax.ShapeDtypeStruct((RES, chans, COLS) if last else sums, jnp.float32),
+        scratch_shapes=([pltpu.VMEM(sums, jnp.float32)] if last else [])
         + [pltpu.VMEM((RES * chans, LANES), jnp.bfloat16)] * 8,
-        compiler_params=pltpu.CompilerParams(vmem_limit_bytes=16 << 20),
+        compiler_params=pltpu.CompilerParams(vmem_limit_bytes=12 << 20),
         name="lags",
-    )(*values, slab, twiddle, high, low)
+    )(*values, slab, twiddle, high, low, *([total] if last else []))
 
 
 def finish_kernel(tiles_ref, out_ref):
@@ -237,8 +266,8 @@
     piece = COLS // RES
     place = lax.broadcasted_iota(jnp.int32, (COLS, COLS), 0)
     lag = lax.broadcasted_iota(jnp.int32, (COLS, COLS), 1)
-    residue = (place // piece - lax.axis_index("win") + RES) % RES
-    order = jnp.where(lag == place % piece * RES + residue, 1.0, 0.0).astype(jnp.bfloat16)
+    residue = ((place >> 5) - lax.axis_index("win") + RES) & (RES - 1)
+    order = jnp.where(lag == (place & (piece - 1)) * RES + residue, 1.0, 0.0).astype(jnp.bfloat16)
     first = total.astype(jnp.bfloat16)
     rest = total - first.astype(jnp.float32)
     second = rest.astype(jnp.bfloat16)
@@ -258,9 +287,9 @@
     )(tiles)
 
 
-def exchange(slab, bit):
+def swap(array, bit):
     peers = lax.axis_size("chan")
-    return slab + lax.ppermute(slab, "chan", [(peer, peer ^ bit) for peer in range(peers)])
+    return lax.ppermute(array, "chan", [(peer, peer ^ bit) for peer in range(peers)])
 
 
 def body(spectra, exponents, source_channels):
@@ -268,13 +297,16 @@
     stay = lambda array: pltpu.with_memory_space_constraint(array, pltpu.MemorySpace.HBM)
     spectra = stay(spectra)
     lanes = stay(jnp.transpose(exponents, (0, 2, 1)))
-    slab = exchange(pick(source_channels, spectra, lanes), 1)
-    slab, first = lax.optimization_barrier((exchange(slab, 16), dequantize(spectra, lanes, 0)))
-    slab = exchange(slab, 2)
-    slab, second = lax.optimization_barrier((exchange(slab, 4), dequantize(spectra, lanes, 1)))
-    slab = exchange(slab, 12)
     tabs = tables(1.0 / math.sqrt(4.0 * F * segs))
-    partial = partial_lags((first, second), slab, tabs)
+    keep, give = pick(source_channels, spectra, lanes)
+    own = keep + swap(give, 1)
+    own, first = lax.optimization_barrier((own + swap(own, 16), dequantize(spectra, lanes, 0)))
+    own = own + swap(own, 2)
+    own, second = lax.optimization_barrier((own + swap(own, 4), dequantize(spectra, lanes, 1)))
+    own = own + swap(own, 12)
+    other = swap(own, 1)
+    total = partial_lags((first, second), own, tabs)
+    partial = partial_lags((first, second), other, tabs, total)
     return finish(lax.all_to_all(partial, "win", 0, 0, tiled=True))[None]
 
 

time: 52.4 us -> 55.8 us (1.065)
  blocking collectives: 17.1 us -> 21.2 us
  waiting for transfers between devices: 7.17 us -> 6.02 us
    all_to_all x1, blocking collectives: 17.1 us -> 21.2 us  [body(): return finish(lax.all_to_all(partial, 'win', 0, 0, tiled=True))[None]]
    ppermute x5 -> x6, waiting for transfers between devices: 7.17 us -> 6.02 us  [swap(): lax.ppermute(array, 'chan', [(peer, peer ^ bit) for peer in range(peers)])]
    pallas_call x1 -> x2, Pallas kernels: 6.36 us -> 6.78 us  [partial_lags(): pl.pallas_call(functools.partial(lags_kernel, last), in_specs=[vmem] * (7...]
    ppermute x5 -> x6, starting transfers between devices: 13.8 us -> 13.5 us  [swap(): lax.ppermute(array, 'chan', [(peer, peer ^ bit) for peer in range(peers)])]
  transfers between devices with their start and end apart: 5 -> 6, of which waited for: 4 -> 4; matrix products, arithmetic and copies ran while one was open for 0% -> 0% of each run, Pallas kernels for 9% -> 14%
where the time goes in v6:
time: 55.8 us; the launch traced here: 55 us
  blocking collectives  21.2 us (38%)
  starting transfers between devices  13.5 us (24%)
  Pallas kernels  13.4 us (24%)
  waiting for transfers between devices  6.02 us (11%)
  between operations  0.79 us (1%)
    all_to_all x1, blocking collectives, body(): return finish(lax.all_to_all(partial, 'win', 0, 0, tiled=True))[None]  21.2 us
    ppermute x6, starting transfers between devices, swap(): lax.ppermute(array, 'chan', [(peer, peer ^ bit) for peer in range(peers)])  13.5 us
    pallas_call x2, Pallas kernels, partial_lags(): pl.pallas_call(functools.partial(lags_kernel, last), in_specs=[vmem] * (7...  6.78 us
    ppermute x6, waiting for transfers between devices, swap(): lax.ppermute(array, 'chan', [(peer, peer ^ bit) for peer in range(peers)])  6.02 us
    pallas_call x2, Pallas kernels, dequantize(): pl.pallas_call(dequantize_kernel, grid=(2,), in_specs=[pl.BlockSpec((1, 1...  4.55 us
    pallas_call x1, Pallas kernels, pick(): pl.pallas_call(pick_kernel, in_specs=[pl.BlockSpec(memory_space=pltpu.SME...  1.2 us
  transfers between devices with their start and end apart: 6, of which 4 were waited for; matrix products, arithmetic and copies ran while one was open for 0% of the time, Pallas kernels for 14%

profile of v6, /device:TPU:4, one launch (start us, length us, event | category | flops | bytes accessed | tf_op | source)
XLA Modules:
  0.0 55.0 jit_solution(12710400230213547475)
XLA Ops:
  0.7 1.2 %pick.1 = (f32[4,2048]{1,0:T(4,128)S(1)}, f32[4,2048]{1,0:T(4,128)S(1)}) custom-call(s32[1]{0:T(128)S(6)} %copy.7.source_ref, bf16[2,2,128,4096]{3,2,1,0:T(8,128)(2,1)} %codes_ref.5, s32[2,32,128]{2,1,0:T(8,128)} %bitcast.2), custom_call_target="tpu_custom_call" | custom-call | tf_op jit(solution)/shard_map/pick/pallas_call | solution.py:107
  1.9 0.1 collective-permute-start
  2.0 1.2 %collective-permute-done = f32[4,2048]{1,0:T(4,128)S(1)} collective-permute-done((f32[4,2048]{1,0:T(4,128)S(1)}, f32[4,2048]{1,0:T(4,128)S(1)}, u32[]{:S(2)}, u32[]{:S(2)}) %collective-permute-start) | collective-permute-done | bytes 32800 | tf_op jit(solution)/shard_map/ppermute | solution.py:292
  3.2 2.3 %collective-permute-start.1 = (f32[4,2048]{1,0:T(4,128)S(1)}, f32[4,2048]{1,0:T(4,128)S(1)}, u32[]{:S(2)}, u32[]{:S(2)}) collective-permute-start(f32[4,2048]{1,0:T(4,128)S(1)} %add.15), channel_id=1, source_target_pairs={{0,128},{8,136},{16,144},{24,152},{32,160},{40,168},{48,176},{56,1... | collective-permute-start | bytes 98312 | tf_op jit(solution)/shard_map/ppermute | solution.py:292
  5.5 2.3 %dequantize.2.first_ref = f32[2,128,4096]{2,1,0:T(8,128)S(1)} custom-call(bf16[2,2,128,4096]{3,2,1,0:T(8,128)(2,1)} %codes_ref.5, s32[2,32,128]{2,1,0:T(8,128)} %bitcast.3), custom_call_target="tpu_custom_call" | custom-call | tf_op jit(solution)/shard_map/dequantize/pallas_call | solution.py:52
  7.7 0.9 %collective-permute-done.1 = f32[4,2048]{1,0:T(4,128)S(1)} collective-permute-done((f32[4,2048]{1,0:T(4,128)S(1)}, f32[4,2048]{1,0:T(4,128)S(1)}, u32[]{:S(2)}, u32[]{:S(2)}) %collective-permute-start.1) | collective-permute-done | bytes 32800 | tf_op jit(solution)/shard_map/ppermute | solution.py:292
  8.7 2.0 %collective-permute-start.2 = (f32[4,2048]{1,0:T(4,128)S(1)}, f32[4,2048]{1,0:T(4,128)S(1)}, u32[]{:S(2)}, u32[]{:S(2)}) collective-permute-start(f32[4,2048]{1,0:T(4,128)S(1)} %add.16), channel_id=1, source_target_pairs={{0,16},{8,24},{16,0},{24,8},{32,48},{40,56},{48,32},{56,40},{64,80... | collective-permute-start | bytes 98312 | tf_op jit(solution)/shard_map/ppermute | solution.py:292
  10.7 2.0 %collective-permute-done.2 = f32[4,2048]{1,0:T(4,128)S(1)} collective-permute-done((f32[4,2048]{1,0:T(4,128)S(1)}, f32[4,2048]{1,0:T(4,128)S(1)}, u32[]{:S(2)}, u32[]{:S(2)}) %collective-permute-start.2) | collective-permute-done | bytes 32800 | tf_op jit(solution)/shard_map/ppermute | solution.py:292
  12.7 0.0 copy-start
  12.7 0.0 copy-start.1
  12.7 0.0 copy-start.2
  12.7 3.4 %collective-permute-start.3 = (f32[4,2048]{1,0:T(4,128)S(1)}, f32[4,2048]{1,0:T(4,128)S(1)}, u32[]{:S(2)}, u32[]{:S(2)}) collective-permute-start(f32[4,2048]{1,0:T(4,128)S(1)} %add.17), channel_id=1, source_target_pairs={{0,32},{8,40},{16,48},{24,56},{32,0},{40,8},{48,16},{56,24},{64,96... | collective-permute-start | bytes 98312 | tf_op jit(solution)/shard_map/ppermute | solution.py:292
  16.1 2.3 %dequantize.3.second_ref = f32[2,128,4096]{2,1,0:T(8,128)S(1)} custom-call(bf16[2,2,128,4096]{3,2,1,0:T(8,128)(2,1)} %codes_ref.5, s32[2,32,128]{2,1,0:T(8,128)} %bitcast.4), custom_call_target="tpu_custom_call" | custom-call | tf_op jit(solution)/shard_map/dequantize/pallas_call | solution.py:52
  18.4 0.0 collective-permute-done.3
  18.4 5.6 %collective-permute-start.4 = (f32[4,2048]{1,0:T(4,128)S(1)}, f32[4,2048]{1,0:T(4,128)S(1)}, u32[]{:S(2)}, u32[]{:S(2)}) collective-permute-start(f32[4,2048]{1,0:T(4,128)S(1)} %add.18), channel_id=1, source_target_pairs={{0,96},{8,104},{16,112},{24,120},{32,64},{40,72},{48,80},{56,88},{... | collective-permute-start | bytes 98312 | tf_op jit(solution)/shard_map/ppermute | solution.py:292
  24.0 1.9 %collective-permute-done.4 = f32[4,2048]{1,0:T(4,128)S(1)} collective-permute-done((f32[4,2048]{1,0:T(4,128)S(1)}, f32[4,2048]{1,0:T(4,128)S(1)}, u32[]{:S(2)}, u32[]{:S(2)}) %collective-permute-start.4) | collective-permute-done | bytes 32800 | tf_op jit(solution)/shard_map/ppermute | solution.py:292
  25.9 0.1 collective-permute-start.5
  26.0 0.0 copy-done
  26.1 0.0 copy-done.1
  26.1 0.0 copy-done.2
  26.1 3.3 %lags.2.refs_0_ = f32[1024,256]{1,0:T(8,128)S(1)} custom-call(f32[2,128,4096]{2,1,0:T(8,128)S(1)} %dequantize.2.first_ref, f32[2,128,4096]{2,1,0:T(8,128)S(1)} %dequantize.3.second_ref, f32[4,2048]{1,0:T(4,128)S(1)} %add.19.slab_ref, f32[16,1024]{1,0:T(8,128)S(1)} %copy-done.2, bf16[2048,256]{1,0:T(8,128)(2,1)S(1)} %copy-done.1, bf16[2048,256]{1,0:T(8,128)(2,1)S(1)} %copy-done), custom_call_target="tpu_custom_call" | custom-call | tf_op jit(solution)/shard_map/lags/pallas_call | solution.py:250
  29.4 0.0 collective-permute-done.5.slab_ref
  29.4 3.5 %lags.3 = f32[8,128,256]{2,1,0:T(8,128)S(1)} custom-call(f32[2,128,4096]{2,1,0:T(8,128)S(1)} %dequantize.2.first_ref, f32[2,128,4096]{2,1,0:T(8,128)S(1)} %dequantize.3.second_ref, f32[4,2048]{1,0:T(4,128)S(1)} %collective-permute-done.5.slab_ref, f32[16,1024]{1,0:T(8,128)S(1)} %copy-done.2, bf16[2048,256]{1,0:T(8,128)(2,1)S(1)} %copy-done.1, ...), custom_call_target="tpu_custom_call" | custom-call | tf_op jit(solution)/shard_map/lags/pallas_call | solution.py:250
  32.9 21.2 %all_to_all.5.tiles_ref = f32[8,128,256]{2,1,0:T(8,128)S(1)} all-to-all(f32[8,128,256]{2,1,0:T(8,128)S(1)} %lags.3), channel_id=1, replica_groups=mesh['chan'=32,'win'=8] {'win'}, dimensions={0} | all-to-all | bytes 2097152 | tf_op jit(solution)/shard_map/all_to_all | solution.py:310
  54.1 0.9 %finish.1 = f32[128,256]{1,0:T(8,128)} custom-call(f32[8,128,256]{2,1,0:T(8,128)S(1)} %all_to_all.5.tiles_ref), custom_call_target="tpu_custom_call" | custom-call | tf_op jit(solution)/shard_map/finish/pallas_call | solution.py:280
  (5 shorter events, 0.1 us)
Async XLA Ops:
  1.9 1.3 %collective-permute-start = (f32[4,2048]{1,0:T(4,128)S(1)}, f32[4,2048]{1,0:T(4,128)S(1)}, u32[]{:S(2)}, u32[]{:S(2)}) collective-permute-start(f32[4,2048]{1,0:T(4,128)S(1)} %get-tuple-element.12), channel_id=1, source_target_pairs={{0,8},{8,0},{16,24},{24,16},{32,40},{40,32},{48,56},{56,48},{64,72... | collective-permute-start | bytes 98312 | tf_op jit(solution)/shard_map/ppermute | solution.py:292
  3.2 5.5 %collective-permute-start.1 = (f32[4,2048]{1,0:T(4,128)S(1)}, f32[4,2048]{1,0:T(4,128)S(1)}, u32[]{:S(2)}, u32[]{:S(2)}) collective-permute-start(f32[4,2048]{1,0:T(4,128)S(1)} %add.15), channel_id=1, source_target_pairs={{0,128},{8,136},{16,144},{24,152},{32,160},{40,168},{48,176},{56,1... | collective-permute-start | bytes 98312 | tf_op jit(solution)/shard_map/ppermute | solution.py:292
  8.7 4.0 %collective-permute-start.2 = (f32[4,2048]{1,0:T(4,128)S(1)}, f32[4,2048]{1,0:T(4,128)S(1)}, u32[]{:S(2)}, u32[]{:S(2)}) collective-permute-start(f32[4,2048]{1,0:T(4,128)S(1)} %add.16), channel_id=1, source_target_pairs={{0,16},{8,24},{16,0},{24,8},{32,48},{40,56},{48,32},{56,40},{64,80... | collective-permute-start | bytes 98312 | tf_op jit(solution)/shard_map/ppermute | solution.py:292
  12.7 13.4 %copy-start = (bf16[2048,256]{1,0:T(8,128)(2,1)S(1)}, bf16[2048,256]{1,0:T(8,128)(2,1)}, u32[]{:S(2)}) copy-start(bf16[2048,256]{1,0:T(8,128)(2,1)} %constant.8.clone.low_ref) | copy-start | bytes 3145732
  12.7 13.3 %copy-start.1 = (bf16[2048,256]{1,0:T(8,128)(2,1)S(1)}, bf16[2048,256]{1,0:T(8,128)(2,1)}, u32[]{:S(2)}) copy-start(bf16[2048,256]{1,0:T(8,128)(2,1)} %constant.7.clone.high_ref) | copy-start | bytes 3145732
  12.7 13.3 %copy-start.2 = (f32[16,1024]{1,0:T(8,128)S(1)}, f32[16,1024]{1,0:T(8,128)}, u32[]{:S(2)}) copy-start(f32[16,1024]{1,0:T(8,128)} %constant.6.clone.twiddle_ref) | copy-start | bytes 196612
  12.7 5.6 %collective-permute-start.3 = (f32[4,2048]{1,0:T(4,128)S(1)}, f32[4,2048]{1,0:T(4,128)S(1)}, u32[]{:S(2)}, u32[]{:S(2)}) collective-permute-start(f32[4,2048]{1,0:T(4,128)S(1)} %add.17), channel_id=1, source_target_pairs={{0,32},{8,40},{16,48},{24,56},{32,0},{40,8},{48,16},{56,24},{64,96... | collective-permute-start | bytes 98312 | tf_op jit(solution)/shard_map/ppermute | solution.py:292
  18.4 7.5 %collective-permute-start.4 = (f32[4,2048]{1,0:T(4,128)S(1)}, f32[4,2048]{1,0:T(4,128)S(1)}, u32[]{:S(2)}, u32[]{:S(2)}) collective-permute-start(f32[4,2048]{1,0:T(4,128)S(1)} %add.18), channel_id=1, source_target_pairs={{0,96},{8,104},{16,112},{24,120},{32,64},{40,72},{48,80},{56,88},{... | collective-permute-start | bytes 98312 | tf_op jit(solution)/shard_map/ppermute | solution.py:292
  25.9 3.5 %collective-permute-start.5 = (f32[4,2048]{1,0:T(4,128)S(1)}, f32[4,2048]{1,0:T(4,128)S(1)}, u32[]{:S(2)}, u32[]{:S(2)}) collective-permute-start(f32[4,2048]{1,0:T(4,128)S(1)} %add.19.slab_ref), channel_id=1, source_target_pairs={{0,8},{8,0},{16,24},{24,16},{32,40},{40,32},{48,56},{56,48},{64,72... | collective-permute-start | bytes 98312 | tf_op jit(solution)/shard_map/ppermute | solution.py:292

commit v7 on v5

--- a/solution.py
+++ b/solution.py
@@ -16,6 +16,7 @@
 LANES = 128
 ROWS = 16
 PIECE = 32
+EIGHT = 8
 ROOT = math.sqrt(0.5)
 
 
@@ -65,13 +66,13 @@
     local = source_ref[0] - lax.axis_index("chan") * chans
     owned = (local >= 0) & (local < chans)
     row = jnp.clip(local, 0, chans - 1)
-    first = pl.multiple_of(row // ROWS * ROWS, ROWS)
-    rows_in = pltpu.make_async_copy(codes_ref.at[:, :, pl.ds(first, ROWS), :], rows_ref, row_sem)
+    first = pl.multiple_of(row // EIGHT * EIGHT, EIGHT)
+    rows_in = pltpu.make_async_copy(codes_ref.at[:, :, pl.ds(first, EIGHT), :], rows_ref, row_sem)
     lanes_in = pltpu.make_async_copy(exponents_ref, lanes_ref, lane_sem)
     rows_in.start()
     lanes_in.start()
     own_lane = lax.broadcasted_iota(jnp.int32, (blocks, chans), 1) == row
-    own_row = lax.broadcasted_iota(jnp.int32, (ROWS, LANES), 0) == row % ROWS
+    own_row = lax.broadcasted_iota(jnp.int32, (EIGHT, LANES), 0) == row % EIGHT
     lanes_in.wait()
     rows_in.wait()
     for g in range(segs):
@@ -95,7 +96,7 @@
         out_specs=pl.BlockSpec(memory_space=pltpu.VMEM),
         out_shape=jax.ShapeDtypeStruct((2 * segs, nbin), jnp.float32),
         scratch_shapes=[
-            pltpu.VMEM((2, segs, ROWS, nbin), jnp.bfloat16),
+            pltpu.VMEM((2, segs, EIGHT, nbin), jnp.bfloat16),
             pltpu.VMEM(lanes.shape, jnp.int32),
             pltpu.SemaphoreType.DMA(()),
             pltpu.SemaphoreType.DMA(()),
@@ -237,8 +238,8 @@
     piece = COLS // RES
     place = lax.broadcasted_iota(jnp.int32, (COLS, COLS), 0)
     lag = lax.broadcasted_iota(jnp.int32, (COLS, COLS), 1)
-    residue = (place // piece - lax.axis_index("win") + RES) % RES
-    order = jnp.where(lag == place % piece * RES + residue, 1.0, 0.0).astype(jnp.bfloat16)
+    residue = ((place >> 5) - lax.axis_index("win") + RES) & (RES - 1)
+    order = jnp.where(lag == (place & (piece - 1)) * RES + residue, 1.0, 0.0).astype(jnp.bfloat16)
     first = total.astype(jnp.bfloat16)
     rest = total - first.astype(jnp.float32)
     second = rest.astype(jnp.bfloat16)
@@ -258,9 +259,10 @@
     )(tiles)
 
 
-def exchange(slab, bit):
+def exchange(slab, *bits):
     peers = lax.axis_size("chan")
-    return slab + lax.ppermute(slab, "chan", [(peer, peer ^ bit) for peer in range(peers)])
+    moved = [lax.ppermute(slab, "chan", [(peer, peer ^ bit) for peer in range(peers)]) for bit in bits]
+    return sum(moved, slab)
 
 
 def body(spectra, exponents, source_channels):
@@ -268,10 +270,10 @@
     stay = lambda array: pltpu.with_memory_space_constraint(array, pltpu.MemorySpace.HBM)
     spectra = stay(spectra)
     lanes = stay(jnp.transpose(exponents, (0, 2, 1)))
-    slab = exchange(pick(source_channels, spectra, lanes), 1)
+    slab = pick(source_channels, spectra, lanes)
+    slab = exchange(slab, 1)
     slab, first = lax.optimization_barrier((exchange(slab, 16), dequantize(spectra, lanes, 0)))
-    slab = exchange(slab, 2)
-    slab, second = lax.optimization_barrier((exchange(slab, 4), dequantize(spectra, lanes, 1)))
+    slab, second = lax.optimization_barrier((exchange(slab, 4, 2, 6), dequantize(spectra, lanes, 1)))
     slab = exchange(slab, 12)
     tabs = tables(1.0 / math.sqrt(4.0 * F * segs))
     partial = partial_lags((first, second), slab, tabs)

time: 52.4 us -> 52 us (level)
  starting transfers between devices: 13.8 us -> 12.4 us
  blocking collectives: 17.1 us -> 17.7 us
    ppermute x5 -> x6, starting transfers between devices: 13.8 us -> 12.4 us  [exchange(): lax.ppermute(slab, 'chan', [(peer, peer ^ bit) for peer in range(peers)])]
    all_to_all x1, blocking collectives: 17.1 us -> 17.7 us  [body(): return finish(lax.all_to_all(partial, 'win', 0, 0, tiled=True))[None]]
    ppermute x5 -> x6, waiting for transfers between devices: 7.17 us -> 7.25 us  [exchange(): lax.ppermute(slab, 'chan', [(peer, peer ^ bit) for peer in range(peers)])]
  transfers between devices with their start and end apart: 5 -> 6, of which waited for: 4 -> 5; matrix products, arithmetic and copies ran while one was open for 0% -> 0% of each run, Pallas kernels for 9% -> 9%
where the time goes in v7:
time: 52 us; the launch traced here: 51.3 us
  blocking collectives  17.7 us (34%)
  Pallas kernels  13 us (25%)
  starting transfers between devices  12.4 us (24%)
  waiting for transfers between devices  7.25 us (14%)
  between operations  0.76 us (1%)
    all_to_all x1, blocking collectives, body(): return finish(lax.all_to_all(partial, 'win', 0, 0, tiled=True))[None]  17.7 us
    ppermute x6, starting transfers between devices, exchange(): lax.ppermute(slab, 'chan', [(peer, peer ^ bit) for peer in range(peers)])  12.4 us
    ppermute x6, waiting for transfers between devices, exchange(): lax.ppermute(slab, 'chan', [(peer, peer ^ bit) for peer in range(peers)])  7.25 us
    pallas_call x1, Pallas kernels, partial_lags(): pl.pallas_call(lags_kernel, in_specs=[vmem] * 6, out_specs=vmem, out_shap...  6.37 us
    pallas_call x2, Pallas kernels, dequantize(): pl.pallas_call(dequantize_kernel, grid=(2,), in_specs=[pl.BlockSpec((1, 1...  4.55 us
    pallas_call x1, Pallas kernels, pick(): pl.pallas_call(pick_kernel, in_specs=[pl.BlockSpec(memory_space=pltpu.SME...  1.19 us
  transfers between devices with their start and end apart: 6, of which 5 were waited for; matrix products, arithmetic and copies ran while one was open for 0% of the time, Pallas kernels for 9%

profile of v7, /device:TPU:4, one launch (start us, length us, event | category | flops | bytes accessed | tf_op | source)
XLA Modules:
  0.0 51.3 jit_solution(1251621941608079102)
XLA Ops:
  0.7 1.2 %pick.1 = f32[4,4096]{1,0:T(4,128)S(1)} custom-call(s32[1]{0:T(128)S(6)} %copy.7.source_ref, bf16[2,2,128,4096]{3,2,1,0:T(8,128)(2,1)} %codes_ref.5, s32[2,32,128]{2,1,0:T(8,128)} %bitcast.2), custom_call_target="tpu_custom_call" | custom-call | tf_op jit(solution)/shard_map/pick/pallas_call | solution.py:93
  1.8 0.1 collective-permute-start
  1.9 1.2 %collective-permute-done = f32[4,4096]{1,0:T(4,128)S(1)} collective-permute-done((f32[4,4096]{1,0:T(4,128)S(1)}, f32[4,4096]{1,0:T(4,128)S(1)}, u32[]{:S(2)}, u32[]{:S(2)}) %collective-permute-start) | collective-permute-done | bytes 65568 | tf_op jit(solution)/shard_map/ppermute | solution.py:264
  3.2 2.3 %collective-permute-start.1 = (f32[4,4096]{1,0:T(4,128)S(1)}, f32[4,4096]{1,0:T(4,128)S(1)}, u32[]{:S(2)}, u32[]{:S(2)}) collective-permute-start(f32[4,4096]{1,0:T(4,128)S(1)} %add.18), channel_id=1, source_target_pairs={{0,128},{8,136},{16,144},{24,152},{32,160},{40,168},{48,176},{56,1... | collective-permute-start | bytes 196616 | tf_op jit(solution)/shard_map/ppermute | solution.py:264
  5.5 2.3 %dequantize.2.first_ref = f32[2,128,4096]{2,1,0:T(8,128)S(1)} custom-call(bf16[2,2,128,4096]{3,2,1,0:T(8,128)(2,1)} %codes_ref.5, s32[2,32,128]{2,1,0:T(8,128)} %bitcast.3), custom_call_target="tpu_custom_call" | custom-call | tf_op jit(solution)/shard_map/dequantize/pallas_call | solution.py:50
  7.8 1.3 %collective-permute-done.1 = f32[4,4096]{1,0:T(4,128)S(1)} collective-permute-done((f32[4,4096]{1,0:T(4,128)S(1)}, f32[4,4096]{1,0:T(4,128)S(1)}, u32[]{:S(2)}, u32[]{:S(2)}) %collective-permute-start.1) | collective-permute-done | bytes 65568 | tf_op jit(solution)/shard_map/ppermute | solution.py:264
  9.1 0.0 copy-start
  9.1 0.0 copy-start.1
  9.1 0.0 copy-start.2
  9.1 4.7 %collective-permute-start.4 = (f32[4,4096]{1,0:T(4,128)S(1)}, f32[4,4096]{1,0:T(4,128)S(1)}, u32[]{:S(2)}, u32[]{:S(2)}) collective-permute-start(f32[4,4096]{1,0:T(4,128)S(1)} %add.19), channel_id=1, source_target_pairs={{0,48},{8,56},{16,32},{24,40},{32,16},{40,24},{48,0},{56,8},{64,11... | collective-permute-start | bytes 196616 | tf_op jit(solution)/shard_map/ppermute | solution.py:264
  13.8 0.0 collective-permute-start.3
  13.8 0.7 %collective-permute-start.2 = (f32[4,4096]{1,0:T(4,128)S(1)}, f32[4,4096]{1,0:T(4,128)S(1)}, u32[]{:S(2)}, u32[]{:S(2)}) collective-permute-start(f32[4,4096]{1,0:T(4,128)S(1)} %add.19), channel_id=1, source_target_pairs={{0,32},{8,40},{16,48},{24,56},{32,0},{40,8},{48,16},{56,24},{64,96... | collective-permute-start | bytes 196616 | tf_op jit(solution)/shard_map/ppermute | solution.py:264
  14.5 2.3 %dequantize.3.second_ref = f32[2,128,4096]{2,1,0:T(8,128)S(1)} custom-call(bf16[2,2,128,4096]{3,2,1,0:T(8,128)(2,1)} %codes_ref.5, s32[2,32,128]{2,1,0:T(8,128)} %bitcast.4), custom_call_target="tpu_custom_call" | custom-call | tf_op jit(solution)/shard_map/dequantize/pallas_call | solution.py:50
  16.8 0.0 collective-permute-done.4
  16.8 1.3 %collective-permute-done.3 = f32[4,4096]{1,0:T(4,128)S(1)} collective-permute-done((f32[4,4096]{1,0:T(4,128)S(1)}, f32[4,4096]{1,0:T(4,128)S(1)}, u32[]{:S(2)}, u32[]{:S(2)}) %collective-permute-start.3) | collective-permute-done | bytes 65568 | tf_op jit(solution)/shard_map/ppermute | solution.py:264
  18.1 0.9 %collective-permute-done.2 = f32[4,4096]{1,0:T(4,128)S(1)} collective-permute-done((f32[4,4096]{1,0:T(4,128)S(1)}, f32[4,4096]{1,0:T(4,128)S(1)}, u32[]{:S(2)}, u32[]{:S(2)}) %collective-permute-start.2) | collective-permute-done | bytes 65568 | tf_op jit(solution)/shard_map/ppermute | solution.py:264
  19.0 4.7 %collective-permute-start.5 = (f32[4,4096]{1,0:T(4,128)S(1)}, f32[4,4096]{1,0:T(4,128)S(1)}, u32[]{:S(2)}, u32[]{:S(2)}) collective-permute-start(f32[4,4096]{1,0:T(4,128)S(1)} %add_add_fusion), channel_id=1, source_target_pairs={{0,96},{8,104},{16,112},{24,120},{32,64},{40,72},{48,80},{56,88},{... | collective-permute-start | bytes 196616 | tf_op jit(solution)/shard_map/ppermute | solution.py:264
  23.7 2.5 %collective-permute-done.5 = f32[4,4096]{1,0:T(4,128)S(1)} collective-permute-done((f32[4,4096]{1,0:T(4,128)S(1)}, f32[4,4096]{1,0:T(4,128)S(1)}, u32[]{:S(2)}, u32[]{:S(2)}) %collective-permute-start.5) | collective-permute-done | bytes 65568 | tf_op jit(solution)/shard_map/ppermute | solution.py:264
  26.3 0.0 copy-done
  26.3 0.0 copy-done.1
  26.3 0.0 copy-done.2
  26.3 6.4 %lags.1 = f32[8,128,256]{2,1,0:T(8,128)S(1)} custom-call(f32[2,128,4096]{2,1,0:T(8,128)S(1)} %dequantize.2.first_ref, f32[2,128,4096]{2,1,0:T(8,128)S(1)} %dequantize.3.second_ref, f32[4,4096]{1,0:T(4,128)S(1)} %add.23.slab_ref, f32[16,1024]{1,0:T(8,128)S(1)} %copy-done.2, bf16[2048,256]{1,0:T(8,128)(2,1)S(1)} %copy-done.1, bf16[2048,256]{1,0:T(8,128)(2,1)S(1)} %copy-done), custom_call_target="tpu_custom_call" | custom-call | tf_op jit(solution)/shard_map/lags/pallas_call | solution.py:222
  32.7 17.7 %all_to_all.5.tiles_ref = f32[8,128,256]{2,1,0:T(8,128)S(1)} all-to-all(f32[8,128,256]{2,1,0:T(8,128)S(1)} %lags.1), channel_id=1, replica_groups=mesh['chan'=32,'win'=8] {'win'}, dimensions={0} | all-to-all | bytes 2097152 | tf_op jit(solution)/shard_map/all_to_all | solution.py:280
  50.4 0.9 %finish.1 = f32[128,256]{1,0:T(8,128)} custom-call(f32[8,128,256]{2,1,0:T(8,128)S(1)} %all_to_all.5.tiles_ref), custom_call_target="tpu_custom_call" | custom-call | tf_op jit(solution)/shard_map/finish/pallas_call | solution.py:252
  (4 shorter events, 0.1 us)
Async XLA Ops:
  1.8 1.3 %collective-permute-start = (f32[4,4096]{1,0:T(4,128)S(1)}, f32[4,4096]{1,0:T(4,128)S(1)}, u32[]{:S(2)}, u32[]{:S(2)}) collective-permute-start(f32[4,4096]{1,0:T(4,128)S(1)} %pick.1), channel_id=1, source_target_pairs={{0,8},{8,0},{16,24},{24,16},{32,40},{40,32},{48,56},{56,48},{64,72... | collective-permute-start | bytes 196616 | tf_op jit(solution)/shard_map/ppermute | solution.py:264
  3.2 5.9 %collective-permute-start.1 = (f32[4,4096]{1,0:T(4,128)S(1)}, f32[4,4096]{1,0:T(4,128)S(1)}, u32[]{:S(2)}, u32[]{:S(2)}) collective-permute-start(f32[4,4096]{1,0:T(4,128)S(1)} %add.18), channel_id=1, source_target_pairs={{0,128},{8,136},{16,144},{24,152},{32,160},{40,168},{48,176},{56,1... | collective-permute-start | bytes 196616 | tf_op jit(solution)/shard_map/ppermute | solution.py:264
  9.1 17.2 %copy-start = (bf16[2048,256]{1,0:T(8,128)(2,1)S(1)}, bf16[2048,256]{1,0:T(8,128)(2,1)}, u32[]{:S(2)}) copy-start(bf16[2048,256]{1,0:T(8,128)(2,1)} %constant.8.clone.low_ref) | copy-start | bytes 3145732
  9.1 17.2 %copy-start.1 = (bf16[2048,256]{1,0:T(8,128)(2,1)S(1)}, bf16[2048,256]{1,0:T(8,128)(2,1)}, u32[]{:S(2)}) copy-start(bf16[2048,256]{1,0:T(8,128)(2,1)} %constant.7.clone.high_ref) | copy-start | bytes 3145732
  9.1 17.2 %copy-start.2 = (f32[16,1024]{1,0:T(8,128)S(1)}, f32[16,1024]{1,0:T(8,128)}, u32[]{:S(2)}) copy-start(f32[16,1024]{1,0:T(8,128)} %constant.6.clone.twiddle_ref) | copy-start | bytes 196612
  9.1 7.7 %collective-permute-start.4 = (f32[4,4096]{1,0:T(4,128)S(1)}, f32[4,4096]{1,0:T(4,128)S(1)}, u32[]{:S(2)}, u32[]{:S(2)}) collective-permute-start(f32[4,4096]{1,0:T(4,128)S(1)} %add.19), channel_id=1, source_target_pairs={{0,48},{8,56},{16,32},{24,40},{32,16},{40,24},{48,0},{56,8},{64,11... | collective-permute-start | bytes 196616 | tf_op jit(solution)/shard_map/ppermute | solution.py:264
  13.8 4.3 %collective-permute-start.3 = (f32[4,4096]{1,0:T(4,128)S(1)}, f32[4,4096]{1,0:T(4,128)S(1)}, u32[]{:S(2)}, u32[]{:S(2)}) collective-permute-start(f32[4,4096]{1,0:T(4,128)S(1)} %add.19), channel_id=1, source_target_pairs={{0,16},{8,24},{16,0},{24,8},{32,48},{40,56},{48,32},{56,40},{64,80... | collective-permute-start | bytes 196616 | tf_op jit(solution)/shard_map/ppermute | solution.py:264
  13.8 5.2 %collective-permute-start.2 = (f32[4,4096]{1,0:T(4,128)S(1)}, f32[4,4096]{1,0:T(4,128)S(1)}, u32[]{:S(2)}, u32[]{:S(2)}) collective-permute-start(f32[4,4096]{1,0:T(4,128)S(1)} %add.19), channel_id=1, source_target_pairs={{0,32},{8,40},{16,48},{24,56},{32,0},{40,8},{48,16},{56,24},{64,96... | collective-permute-start | bytes 196616 | tf_op jit(solution)/shard_map/ppermute | solution.py:264
  19.0 7.2 %collective-permute-start.5 = (f32[4,4096]{1,0:T(4,128)S(1)}, f32[4,4096]{1,0:T(4,128)S(1)}, u32[]{:S(2)}, u32[]{:S(2)}) collective-permute-start(f32[4,4096]{1,0:T(4,128)S(1)} %add_add_fusion), channel_id=1, source_target_pairs={{0,96},{8,104},{16,112},{24,120},{32,64},{40,72},{48,80},{56,88},{... | collective-permute-start | bytes 196616 | tf_op jit(solution)/shard_map/ppermute | solution.py:264

commit v8 on v7

--- a/solution.py
+++ b/solution.py
@@ -67,24 +67,28 @@
     owned = (local >= 0) & (local < chans)
     row = jnp.clip(local, 0, chans - 1)
     first = pl.multiple_of(row // EIGHT * EIGHT, EIGHT)
-    rows_in = pltpu.make_async_copy(codes_ref.at[:, :, pl.ds(first, EIGHT), :], rows_ref, row_sem)
-    lanes_in = pltpu.make_async_copy(exponents_ref, lanes_ref, lane_sem)
-    rows_in.start()
-    lanes_in.start()
-    own_lane = lax.broadcasted_iota(jnp.int32, (blocks, chans), 1) == row
-    own_row = lax.broadcasted_iota(jnp.int32, (EIGHT, LANES), 0) == row % EIGHT
-    lanes_in.wait()
-    rows_in.wait()
-    for g in range(segs):
-        exponent = jnp.sum(jnp.where(own_lane, lanes_ref[g].astype(jnp.float32), 0.0), axis=1, keepdims=True)
-        scale = jnp.where(owned, jnp.exp2(exponent), 0.0)
-        scale = jnp.broadcast_to(scale, (blocks, LANES)).astype(jnp.bfloat16).astype(jnp.float32)
-        for part in range(2):
-            for block in range(blocks):
-                at = pl.ds(block * LANES, LANES)
-                codes = rows_ref[part, g, :, at].astype(jnp.float32)
-                code = jnp.sum(jnp.where(own_row, codes, 0.0), axis=0, keepdims=True)
-                slab_ref[pl.ds(part * segs + g, 1), at] = code * scale[block : block + 1]
+    slab_ref[...] = jnp.zeros_like(slab_ref)
+
+    @pl.when(owned)
+    def _():
+        rows_in = pltpu.make_async_copy(codes_ref.at[:, :, pl.ds(first, EIGHT), :], rows_ref, row_sem)
+        lanes_in = pltpu.make_async_copy(exponents_ref, lanes_ref, lane_sem)
+        rows_in.start()
+        lanes_in.start()
+        own_lane = lax.broadcasted_iota(jnp.int32, (blocks, chans), 1) == row
+        own_row = lax.broadcasted_iota(jnp.int32, (EIGHT, LANES), 0) == row % EIGHT
+        lanes_in.wait()
+        rows_in.wait()
+        for g in range(segs):
+            exponent = jnp.sum(jnp.where(own_lane, lanes_ref[g].astype(jnp.float32), 0.0), axis=1, keepdims=True)
+            scale = jnp.exp2(exponent)
+            scale = jnp.broadcast_to(scale, (blocks, LANES)).astype(jnp.bfloat16).astype(jnp.float32)
+            for part in range(2):
+                for block in range(blocks):
+                    at = pl.ds(block * LANES, LANES)
+                    codes = rows_ref[part, g, :, at].astype(jnp.float32)
+                    code = jnp.sum(jnp.where(own_row, codes, 0.0), axis=0, keepdims=True)
+                    slab_ref[pl.ds(part * segs + g, 1), at] = code * scale[block : block + 1]
 
 
 def pick(source_channels, spectra, lanes):

time: 52 us -> 51.2 us (0.985)
  Pallas kernels: 13 us -> 11.9 us
    pallas_call x1, Pallas kernels: 1.19 us -> 0.04 us  [pick(): pl.pallas_call(pick_kernel, in_specs=[pl.BlockSpec(memory_space=pltpu.SME...]
where the time goes in v8:
time: 51.2 us; the launch traced here: 50.9 us
  blocking collectives  18.1 us (35%)
  starting transfers between devices  12.8 us (25%)
  Pallas kernels  11.9 us (23%)
  waiting for transfers between devices  7.25 us (14%)
  between operations  0.76 us (1%)
    all_to_all x1, blocking collectives, body(): return finish(lax.all_to_all(partial, 'win', 0, 0, tiled=True))[None]  18.1 us
    ppermute x6, starting transfers between devices, exchange(): lax.ppermute(slab, 'chan', [(peer, peer ^ bit) for peer in range(peers)])  12.8 us
    ppermute x6, waiting for transfers between devices, exchange(): lax.ppermute(slab, 'chan', [(peer, peer ^ bit) for peer in range(peers)])  7.25 us
    pallas_call x1, Pallas kernels, partial_lags(): pl.pallas_call(lags_kernel, in_specs=[vmem] * 6, out_specs=vmem, out_shap...  6.36 us
    pallas_call x2, Pallas kernels, dequantize(): pl.pallas_call(dequantize_kernel, grid=(2,), in_specs=[pl.BlockSpec((1, 1...  4.55 us
  transfers between devices with their start and end apart: 6, of which 5 were waited for; matrix products, arithmetic and copies ran while one was open for 0% of the time, Pallas kernels for 9%

profile of v8, /device:TPU:4, one launch (start us, length us, event | category | flops | bytes accessed | tf_op | source)
XLA Modules:
  0.0 50.9 jit_solution(1910718631603827410)
XLA Ops:
  0.7 0.1 collective-permute-start
  0.8 1.2 %collective-permute-done = f32[4,4096]{1,0:T(4,128)S(1)} collective-permute-done((f32[4,4096]{1,0:T(4,128)S(1)}, f32[4,4096]{1,0:T(4,128)S(1)}, u32[]{:S(2)}, u32[]{:S(2)}) %collective-permute-start) | collective-permute-done | bytes 65568 | tf_op jit(solution)/shard_map/ppermute | solution.py:268
  2.1 2.3 %collective-permute-start.1 = (f32[4,4096]{1,0:T(4,128)S(1)}, f32[4,4096]{1,0:T(4,128)S(1)}, u32[]{:S(2)}, u32[]{:S(2)}) collective-permute-start(f32[4,4096]{1,0:T(4,128)S(1)} %add.18), channel_id=1, source_target_pairs={{0,128},{8,136},{16,144},{24,152},{32,160},{40,168},{48,176},{56,1... | collective-permute-start | bytes 196616 | tf_op jit(solution)/shard_map/ppermute | solution.py:268
  4.4 2.3 %dequantize.2.first_ref = f32[2,128,4096]{2,1,0:T(8,128)S(1)} custom-call(bf16[2,2,128,4096]{3,2,1,0:T(8,128)(2,1)} %codes_ref.5, s32[2,32,128]{2,1,0:T(8,128)} %bitcast.3), custom_call_target="tpu_custom_call" | custom-call | tf_op jit(solution)/shard_map/dequantize/pallas_call | solution.py:50
  6.6 1.3 %collective-permute-done.1 = f32[4,4096]{1,0:T(4,128)S(1)} collective-permute-done((f32[4,4096]{1,0:T(4,128)S(1)}, f32[4,4096]{1,0:T(4,128)S(1)}, u32[]{:S(2)}, u32[]{:S(2)}) %collective-permute-start.1) | collective-permute-done | bytes 65568 | tf_op jit(solution)/shard_map/ppermute | solution.py:268
  7.9 0.0 copy-start
  8.0 0.0 copy-start.1
  8.0 0.0 copy-start.2
  8.0 4.7 %collective-permute-start.4 = (f32[4,4096]{1,0:T(4,128)S(1)}, f32[4,4096]{1,0:T(4,128)S(1)}, u32[]{:S(2)}, u32[]{:S(2)}) collective-permute-start(f32[4,4096]{1,0:T(4,128)S(1)} %add.19), channel_id=1, source_target_pairs={{0,48},{8,56},{16,32},{24,40},{32,16},{40,24},{48,0},{56,8},{64,11... | collective-permute-start | bytes 196616 | tf_op jit(solution)/shard_map/ppermute | solution.py:268
  12.7 0.0 collective-permute-start.3
  12.7 0.7 %collective-permute-start.2 = (f32[4,4096]{1,0:T(4,128)S(1)}, f32[4,4096]{1,0:T(4,128)S(1)}, u32[]{:S(2)}, u32[]{:S(2)}) collective-permute-start(f32[4,4096]{1,0:T(4,128)S(1)} %add.19), channel_id=1, source_target_pairs={{0,32},{8,40},{16,48},{24,56},{32,0},{40,8},{48,16},{56,24},{64,96... | collective-permute-start | bytes 196616 | tf_op jit(solution)/shard_map/ppermute | solution.py:268
  13.4 2.3 %dequantize.3.second_ref = f32[2,128,4096]{2,1,0:T(8,128)S(1)} custom-call(bf16[2,2,128,4096]{3,2,1,0:T(8,128)(2,1)} %codes_ref.5, s32[2,32,128]{2,1,0:T(8,128)} %bitcast.4), custom_call_target="tpu_custom_call" | custom-call | tf_op jit(solution)/shard_map/dequantize/pallas_call | solution.py:50
  15.6 0.0 collective-permute-done.4
  15.6 1.3 %collective-permute-done.3 = f32[4,4096]{1,0:T(4,128)S(1)} collective-permute-done((f32[4,4096]{1,0:T(4,128)S(1)}, f32[4,4096]{1,0:T(4,128)S(1)}, u32[]{:S(2)}, u32[]{:S(2)}) %collective-permute-start.3) | collective-permute-done | bytes 65568 | tf_op jit(solution)/shard_map/ppermute | solution.py:268
  17.0 0.9 %collective-permute-done.2 = f32[4,4096]{1,0:T(4,128)S(1)} collective-permute-done((f32[4,4096]{1,0:T(4,128)S(1)}, f32[4,4096]{1,0:T(4,128)S(1)}, u32[]{:S(2)}, u32[]{:S(2)}) %collective-permute-start.2) | collective-permute-done | bytes 65568 | tf_op jit(solution)/shard_map/ppermute | solution.py:268
  17.9 5.1 %collective-permute-start.5 = (f32[4,4096]{1,0:T(4,128)S(1)}, f32[4,4096]{1,0:T(4,128)S(1)}, u32[]{:S(2)}, u32[]{:S(2)}) collective-permute-start(f32[4,4096]{1,0:T(4,128)S(1)} %add_add_fusion), channel_id=1, source_target_pairs={{0,96},{8,104},{16,112},{24,120},{32,64},{40,72},{48,80},{56,88},{... | collective-permute-start | bytes 196616 | tf_op jit(solution)/shard_map/ppermute | solution.py:268
  23.0 2.5 %collective-permute-done.5 = f32[4,4096]{1,0:T(4,128)S(1)} collective-permute-done((f32[4,4096]{1,0:T(4,128)S(1)}, f32[4,4096]{1,0:T(4,128)S(1)}, u32[]{:S(2)}, u32[]{:S(2)}) %collective-permute-start.5) | collective-permute-done | bytes 65568 | tf_op jit(solution)/shard_map/ppermute | solution.py:268
  25.5 0.0 copy-done
  25.5 0.0 copy-done.1
  25.5 0.0 copy-done.2
  25.5 6.4 %lags.1 = f32[8,128,256]{2,1,0:T(8,128)S(1)} custom-call(f32[2,128,4096]{2,1,0:T(8,128)S(1)} %dequantize.2.first_ref, f32[2,128,4096]{2,1,0:T(8,128)S(1)} %dequantize.3.second_ref, f32[4,4096]{1,0:T(4,128)S(1)} %add.23.slab_ref, f32[16,1024]{1,0:T(8,128)S(1)} %copy-done.2, bf16[2048,256]{1,0:T(8,128)(2,1)S(1)} %copy-done.1, bf16[2048,256]{1,0:T(8,128)(2,1)S(1)} %copy-done), custom_call_target="tpu_custom_call" | custom-call | tf_op jit(solution)/shard_map/lags/pallas_call | solution.py:226
  31.9 18.1 %all_to_all.5.tiles_ref = f32[8,128,256]{2,1,0:T(8,128)S(1)} all-to-all(f32[8,128,256]{2,1,0:T(8,128)S(1)} %lags.1), channel_id=1, replica_groups=mesh['chan'=32,'win'=8] {'win'}, dimensions={0} | all-to-all | bytes 2097152 | tf_op jit(solution)/shard_map/all_to_all | solution.py:284
  50.0 0.9 %finish.1 = f32[128,256]{1,0:T(8,128)} custom-call(f32[8,128,256]{2,1,0:T(8,128)S(1)} %all_to_all.5.tiles_ref), custom_call_target="tpu_custom_call" | custom-call | tf_op jit(solution)/shard_map/finish/pallas_call | solution.py:256
  (5 shorter events, 0.1 us)
Async XLA Ops:
  0.7 1.3 %collective-permute-start = (f32[4,4096]{1,0:T(4,128)S(1)}, f32[4,4096]{1,0:T(4,128)S(1)}, u32[]{:S(2)}, u32[]{:S(2)}) collective-permute-start(f32[4,4096]{1,0:T(4,128)S(1)} %pick.1), channel_id=1, source_target_pairs={{0,8},{8,0},{16,24},{24,16},{32,40},{40,32},{48,56},{56,48},{64,72... | collective-permute-start | bytes 196616 | tf_op jit(solution)/shard_map/ppermute | solution.py:268
  2.1 5.9 %collective-permute-start.1 = (f32[4,4096]{1,0:T(4,128)S(1)}, f32[4,4096]{1,0:T(4,128)S(1)}, u32[]{:S(2)}, u32[]{:S(2)}) collective-permute-start(f32[4,4096]{1,0:T(4,128)S(1)} %add.18), channel_id=1, source_target_pairs={{0,128},{8,136},{16,144},{24,152},{32,160},{40,168},{48,176},{56,1... | collective-permute-start | bytes 196616 | tf_op jit(solution)/shard_map/ppermute | solution.py:268
  7.9 17.6 %copy-start = (bf16[2048,256]{1,0:T(8,128)(2,1)S(1)}, bf16[2048,256]{1,0:T(8,128)(2,1)}, u32[]{:S(2)}) copy-start(bf16[2048,256]{1,0:T(8,128)(2,1)} %constant.8.clone.low_ref) | copy-start | bytes 3145732
  8.0 17.6 %copy-start.1 = (bf16[2048,256]{1,0:T(8,128)(2,1)S(1)}, bf16[2048,256]{1,0:T(8,128)(2,1)}, u32[]{:S(2)}) copy-start(bf16[2048,256]{1,0:T(8,128)(2,1)} %constant.7.clone.high_ref) | copy-start | bytes 3145732
  8.0 17.6 %copy-start.2 = (f32[16,1024]{1,0:T(8,128)S(1)}, f32[16,1024]{1,0:T(8,128)}, u32[]{:S(2)}) copy-start(f32[16,1024]{1,0:T(8,128)} %constant.6.clone.twiddle_ref) | copy-start | bytes 196612
  8.0 7.7 %collective-permute-start.4 = (f32[4,4096]{1,0:T(4,128)S(1)}, f32[4,4096]{1,0:T(4,128)S(1)}, u32[]{:S(2)}, u32[]{:S(2)}) collective-permute-start(f32[4,4096]{1,0:T(4,128)S(1)} %add.19), channel_id=1, source_target_pairs={{0,48},{8,56},{16,32},{24,40},{32,16},{40,24},{48,0},{56,8},{64,11... | collective-permute-start | bytes 196616 | tf_op jit(solution)/shard_map/ppermute | solution.py:268
  12.7 4.3 %collective-permute-start.3 = (f32[4,4096]{1,0:T(4,128)S(1)}, f32[4,4096]{1,0:T(4,128)S(1)}, u32[]{:S(2)}, u32[]{:S(2)}) collective-permute-start(f32[4,4096]{1,0:T(4,128)S(1)} %add.19), channel_id=1, source_target_pairs={{0,16},{8,24},{16,0},{24,8},{32,48},{40,56},{48,32},{56,40},{64,80... | collective-permute-start | bytes 196616 | tf_op jit(solution)/shard_map/ppermute | solution.py:268
  12.7 5.2 %collective-permute-start.2 = (f32[4,4096]{1,0:T(4,128)S(1)}, f32[4,4096]{1,0:T(4,128)S(1)}, u32[]{:S(2)}, u32[]{:S(2)}) collective-permute-start(f32[4,4096]{1,0:T(4,128)S(1)} %add.19), channel_id=1, source_target_pairs={{0,32},{8,40},{16,48},{24,56},{32,0},{40,8},{48,16},{56,24},{64,96... | collective-permute-start | bytes 196616 | tf_op jit(solution)/shard_map/ppermute | solution.py:268
  17.9 7.6 %collective-permute-start.5 = (f32[4,4096]{1,0:T(4,128)S(1)}, f32[4,4096]{1,0:T(4,128)S(1)}, u32[]{:S(2)}, u32[]{:S(2)}) collective-permute-start(f32[4,4096]{1,0:T(4,128)S(1)} %add_add_fusion), channel_id=1, source_target_pairs={{0,96},{8,104},{16,112},{24,120},{32,64},{40,72},{48,80},{56,88},{... | collective-permute-start | bytes 196616 | tf_op jit(solution)/shard_map/ppermute | solution.py:268
